TPU v7x, 256 devices: a whole 4x4x8 slice. The times are simulated.
256 devices in a mesh: seq: 64 (over y, z, core), head: 4 (over x).
Axes of the slice: x: 4, y: 4, z: 8, core: 2. Of those that a mesh axis runs over, the one named last changes fastest.
Arguments:
- queries: bfloat16 [65536, 512], P('seq', 'head'), may hold values from -6 to 6
- keys: bfloat16 [65536, 512], P('seq', 'head'), may hold values from -6 to 6
- values: bfloat16 [65536, 512], P('seq', 'head'), may hold values from -6 to 6
- outputs: bfloat16 [65536, 512], P('seq', 'head'), may hold values from -6 to 6
- d_outputs: bfloat16 [65536, 512], P('seq', 'head'), may hold values from -6 to 6
- log_norm: float32 [8, 65536], P('head', 'seq'), may hold values from 4 to 5.5
- rand_owner: int32 [512, 3], P('seq'), may hold values from 0 to 63, all different within a row; in each aligned block of 8 rows (0 to 7, 8 to 15, ...) at most 2 rows name the same one
- rand_local: int32 [512, 3], P('seq'), may hold values from 0 to 7
- glob_blocks: int32 [2], replicated, may hold values from 0 to 511
Outputs:
- d_queries: bfloat16 [65536, 512], P('seq', 'head')
- d_keys: bfloat16 [65536, 512], P('seq', 'head')
- d_values: bfloat16 [65536, 512], P('seq', 'head')
Inputs may be any that keep to these rules, and one draw needn't show every extreme that they name: `rand_owner`: each row names 3 different seq indices; within the 8 rows of one seq index no value is named more than 2 times, a bound that some block reaches.
All inputs are finite; a program needn't handle non-finite values.
Results may differ from a plain program's by a relative error of at most 0.0085.
Values may be sent and summed in bfloat16 or wider, within the bound.
A program may use at most 128 MiB of HBM per device.

v0:
```python
import math

import jax
import jax.numpy as jnp
from jax import lax
from jax.sharding import PartitionSpec as P

BLOCK = 128


def extended(array, sides, width):
    for axis, dim in sides:
        size, length = (lax.axis_size(axis), array.shape[dim])
        up = [(i, (i + 1) % size) for i in range(size - 1)]
        down = [(j, i) for i, j in up]
        last = lax.slice_in_dim(array, length - width, length, axis=dim)
        leading = lax.slice_in_dim(array, 0, width, axis=dim)
        before = lax.ppermute(last, axis, up)
        after = lax.ppermute(leading, axis, down)
        array = jnp.concatenate([before, array, after], axis=dim)
    return array


def pair_terms(query_rows, grad_rows, norm_rows, delta_rows, key_rows, value_rows, factor):
    scores = (
        jnp.einsum("nqhd,nkhd->nhqk", query_rows, key_rows, preferred_element_type=jnp.float32)
        * factor
    )
    weights = jnp.exp(scores - norm_rows[..., None])
    grad_weights = jnp.einsum(
        "nqhd,nkhd->nhqk", grad_rows, value_rows, preferred_element_type=jnp.float32
    )
    grad_scores = weights * (grad_weights - delta_rows[..., None])
    weights_low = weights.astype(jnp.bfloat16)
    scores_low = grad_scores.astype(jnp.bfloat16)
    grad_query = (
        jnp.einsum("nhqk,nkhd->nqhd", scores_low, key_rows, preferred_element_type=jnp.float32)
        * factor
    )
    grad_key = (
        jnp.einsum("nhqk,nqhd->nkhd", scores_low, query_rows, preferred_element_type=jnp.float32)
        * factor
    )
    grad_value = jnp.einsum(
        "nhqk,nqhd->nkhd", weights_low, grad_rows, preferred_element_type=jnp.float32
    )
    return (grad_query, grad_key, grad_value)


def add_by_block(targets, block_ids, blocks):
    selector = (block_ids[:, None] == jnp.arange(blocks, dtype=jnp.int32)[None, :]).astype(
        jnp.bfloat16
    )
    flat_terms = targets.reshape(targets.shape[0], -1)
    high_part = flat_terms.astype(jnp.bfloat16)
    low_part = (flat_terms - high_part.astype(jnp.float32)).astype(jnp.bfloat16)
    summed = jnp.einsum("sn,sf->nf", selector, high_part, preferred_element_type=jnp.float32)
    summed = summed + jnp.einsum(
        "sn,sf->nf", selector, low_part, preferred_element_type=jnp.float32
    )
    return summed.reshape((blocks,) + targets.shape[1:])


def shards(
    queries, keys, values, outputs, d_outputs, log_norm, rand_owner, rand_local, glob_blocks
):
    tokens_here, features = queries.shape
    heads_here = log_norm.shape[0]
    head_size = features // heads_here
    blocks = tokens_here // BLOCK
    per_block = rand_owner.shape[1]
    factor = 1.0 / math.sqrt(head_size)
    owners = lax.axis_size("seq")
    seq_index = lax.axis_index("seq")
    block_shape = (blocks, BLOCK, heads_here, head_size)
    query_blocks = queries.reshape(block_shape)
    grad_blocks = d_outputs.reshape(block_shape)
    split_out = outputs.reshape(tokens_here, heads_here, head_size).astype(jnp.float32)
    split_grad = d_outputs.reshape(tokens_here, heads_here, head_size).astype(jnp.float32)
    delta_flat = jnp.sum(split_out * split_grad, axis=-1).T
    delta_blocks = delta_flat.reshape(heads_here, blocks, BLOCK).transpose(1, 0, 2)
    norm_blocks = log_norm.reshape(heads_here, blocks, BLOCK).transpose(1, 0, 2)
    d_queries = jnp.zeros(block_shape, jnp.float32)
    pad_shape = (blocks + 2,) + block_shape[1:]
    keys_grad_pad = jnp.zeros(pad_shape, jnp.float32)
    values_grad_pad = jnp.zeros(pad_shape, jnp.float32)
    padded = extended(jnp.stack([keys, values]), (("seq", 1),), BLOCK)
    keys_pad = padded[0].reshape(pad_shape)
    values_pad = padded[1].reshape(pad_shape)
    for offset in range(3):
        grad_query, grad_key, grad_value = pair_terms(
            query_blocks,
            grad_blocks,
            norm_blocks,
            delta_blocks,
            keys_pad[offset : offset + blocks],
            values_pad[offset : offset + blocks],
            factor,
        )
        d_queries = d_queries + grad_query
        keys_grad_pad = keys_grad_pad.at[offset : offset + blocks].add(grad_key)
        values_grad_pad = values_grad_pad.at[offset : offset + blocks].add(grad_value)
    outgoing_edges = jnp.stack(
        [
            jnp.concatenate([keys_grad_pad[0], keys_grad_pad[blocks + 1]], axis=0).reshape(
                2 * BLOCK, features
            ),
            jnp.concatenate([values_grad_pad[0], values_grad_pad[blocks + 1]], axis=0).reshape(
                2 * BLOCK, features
            ),
        ]
    )
    arrived = extended(outgoing_edges.astype(jnp.bfloat16), (("seq", 1),), BLOCK).astype(
        outgoing_edges.dtype
    )
    from_before = arrived[:, :BLOCK].reshape((2,) + block_shape[1:])
    from_after = arrived[:, 3 * BLOCK :].reshape((2,) + block_shape[1:])
    d_keys = (
        keys_grad_pad[1 : blocks + 1].at[0].add(from_before[0]).at[blocks - 1].add(from_after[0])
    )
    d_values = (
        values_grad_pad[1 : blocks + 1].at[0].add(from_before[1]).at[blocks - 1].add(from_after[1])
    )
    global_owner = glob_blocks // blocks
    global_local = glob_blocks % blocks
    owned_here = (global_owner == seq_index).astype(jnp.float32)
    key_table = keys.reshape(blocks, BLOCK, features)
    value_table = values.reshape(blocks, BLOCK, features)
    own_part = jnp.stack([key_table[global_local], value_table[global_local]], axis=1).astype(
        jnp.float32
    )
    own_part = own_part * owned_here[:, None, None, None]
    shared = lax.psum(own_part, "seq").astype(jnp.bfloat16)
    global_pieces = []
    for number in range(shared.shape[0]):
        key_rows = jnp.broadcast_to(shared[number, 0].reshape(block_shape[1:]), block_shape)
        value_rows = jnp.broadcast_to(shared[number, 1].reshape(block_shape[1:]), block_shape)
        grad_query, grad_key, grad_value = pair_terms(
            query_blocks, grad_blocks, norm_blocks, delta_blocks, key_rows, value_rows, factor
        )
        d_queries = d_queries + grad_query
        global_pieces.append(
            jnp.stack(
                [
                    jnp.sum(grad_key, axis=0).reshape(BLOCK, features),
                    jnp.sum(grad_value, axis=0).reshape(BLOCK, features),
                ]
            )
        )
    totals = lax.psum(jnp.stack(global_pieces), "seq")
    for number in range(shared.shape[0]):
        d_keys = d_keys.at[global_local[number]].add(
            owned_here[number] * totals[number, 0].reshape(block_shape[1:])
        )
        d_values = d_values.at[global_local[number]].add(
            owned_here[number] * totals[number, 1].reshape(block_shape[1:])
        )
    references = blocks * per_block
    capacity = max(2, (references + owners - 1) // owners)
    owner_flat = rand_owner.reshape(-1)
    local_flat = rand_local.reshape(-1)
    matches = (owner_flat[:, None] == jnp.arange(owners, dtype=jnp.int32)[None, :]).astype(
        jnp.int32
    )
    within = jnp.sum((jnp.cumsum(matches, axis=0) - 1) * matches, axis=1)
    slot_index = owner_flat * capacity + within
    requested = jnp.zeros((owners * capacity,), jnp.int32).at[slot_index].set(local_flat)
    wanted = lax.all_to_all(
        requested.reshape(owners, capacity), "seq", split_axis=0, concat_axis=0, tiled=True
    )
    wanted_flat = wanted.reshape(-1)
    outgoing = jnp.stack([key_table[wanted_flat], value_table[wanted_flat]], axis=1)
    fetched = lax.all_to_all(
        outgoing.reshape(owners, capacity, 2, BLOCK, features),
        "seq",
        split_axis=0,
        concat_axis=0,
        tiled=True,
    )
    picked = fetched.reshape(owners * capacity, 2, BLOCK, features)[slot_index]
    picked = picked.reshape((blocks, per_block, 2) + block_shape[1:])
    pieces = []
    for column in range(per_block):
        grad_query, grad_key, grad_value = pair_terms(
            query_blocks,
            grad_blocks,
            norm_blocks,
            delta_blocks,
            picked[:, column, 0],
            picked[:, column, 1],
            factor,
        )
        d_queries = d_queries + grad_query
        pieces.append(jnp.stack([grad_key, grad_value], axis=1))
    partials = jnp.stack(pieces, axis=1).reshape(references, 2, BLOCK, features)
    returned = (
        jnp.zeros((owners * capacity, 2, BLOCK, features), jnp.float32).at[slot_index].set(partials)
    )
    received = lax.all_to_all(
        returned.reshape(owners, capacity, 2, BLOCK, features).astype(jnp.bfloat16),
        "seq",
        split_axis=0,
        concat_axis=0,
        tiled=True,
    ).astype(jnp.float32)
    summed = add_by_block(
        received.reshape(owners * capacity, 2, BLOCK, features), wanted_flat, blocks
    )
    d_keys = d_keys + summed[:, 0].reshape(block_shape)
    d_values = d_values + summed[:, 1].reshape(block_shape)
    return (
        d_queries.reshape(tokens_here, features).astype(jnp.bfloat16),
        d_keys.reshape(tokens_here, features).astype(jnp.bfloat16),
        d_values.reshape(tokens_here, features).astype(jnp.bfloat16),
    )


def solution(mesh):
    placed = (
        P("seq", "head"),
        P("seq", "head"),
        P("seq", "head"),
        P("seq", "head"),
        P("seq", "head"),
        P("head", "seq"),
        P("seq", None),
        P("seq", None),
        P(),
    )
    return jax.shard_map(
        shards,
        mesh=mesh,
        in_specs=placed,
        out_specs=(P("seq", "head"), P("seq", "head"), P("seq", "head")),
        check_vma=False,
    )
```

profile of v0, /device:TPU:1, one launch (start us, length us, event | category | flops | bytes accessed | tf_op | source)
XLA Modules:
  0.0 938.6 jit_solution(7537119073880668998)
XLA Ops:
  10.9 22.2 %all_to_all.19 = s32[64,1,2]{2,1,0:T(1,128)S(1)} all-to-all(s32[64,1,2]{2,1,0:T(1,128)S(1)} %bitcast.340), channel_id=1, replica_groups=mesh['seq'=64,'head'=4] {'seq'}, dimensions={0} | all-to-all | bytes 1024 | tf_op jit(solution)/shard_map/all_to_all | solution.py:168
  34.5 3.1 gather_fusion.3
  37.6 3.0 gather_fusion.2
  40.6 7.5 pad_maximum_fusion
  48.1 5.9 all-to-all-start.1
  55.2 184.7 %all-to-all-done.1 = bf16[64,2,2,128,128]{4,3,1,2,0:T(8,128)(2,1)} async-done(((bf16[64,2,2,128,128]{4,3,1,2,0:T(8,128)(2,1)}), bf16[64,2,2,128,128]{4,3,1,2,0:T(8,128)(2,1)}, u32[]{:S(2)}, u32[]{:S(2)}) %all-to-all-start.1) | async-done | bytes 8388640 | tf_op jit(solution)/shard_map/all_to_all | solution.py:173
  239.8 10.3 %copy.256 = bf16[64,2,2,128,128]{4,3,2,1,0:T(8,128)(2,1)} copy(bf16[64,2,2,128,128]{4,3,1,2,0:T(8,128)(2,1)} %all-to-all-done.1) | data formatting | bytes 16777216 | tf_op jit(solution)/shard_map/all_to_all | solution.py:173
  250.2 5.4 gather_fusion.4
  255.6 1.9 copy.257
  263.3 1.9 copy.289
  265.2 3.5 copy.290
  268.7 7.9 broadcast_in_dim.17
  276.6 7.7 scatter_fusion
  284.3 9.2 convert_element_type.120
  293.5 6.3 all-to-all-start.2
  300.5 3.5 collective-permute-start
  304.1 1.9 collective-permute-start.1
  307.3 409.5 %all-reduce.6 = bf16[2,2,128,128]{3,2,0,1:T(8,128)(2,1)S(1)} all-reduce(f32[2,2,128,128]{3,2,0,1:T(8,128)S(1)} %convert_multiply_fusion.1), channel_id=1, replica_groups=mesh['seq'=64,'head'=4] {'seq'}, use_global_device_ids=true, to_apply=%region_1.0 | all-reduce | flops 65536 | bytes 393216 | tf_op jit(solution)/shard_map/psum | solution.py:133
  730.8 2.1 convolution_bitcast_fusion.10
  735.9 1.3 convolution_bitcast_fusion.12
  737.9 1.7 pad_maximum_fusion.5
  748.2 3.6 collective-permute-start.2
  751.9 5.6 collective-permute-start.3
  760.5 1.5 fusion.80
  761.9 133.5 %all-reduce.5.cloned.1.call-done = f32[2,2,128,128]{2,3,1,0:T(8,128)} async-done(((f32[2,2,128,128]{2,3,1,0:T(8,128)}), f32[2,2,128,128]{2,3,1,0:T(8,128)}) %all-reduce.5.cloned.1.call-update) | async-done | bytes 262160 | tf_op jit(solution)/shard_map/psum | solution.py:150
  895.4 2.3 slice_multiply_fusion
  897.8 2.1 fusion.76
  899.9 2.1 fusion.77
  902.0 2.1 fusion.79
  906.7 13.3 %reshape_reshape.6 = bf16[128,32768]{1,0:T(8,128)(2,1)} reshape(bf16[64,2,2,128,128]{4,3,2,1,0:T(8,128)(2,1)} %all-to-all-done.2) | data formatting | bytes 16777216 | tf_op jit(solution)/shard_map/reshape;reshape | solution.py:54
  920.0 4.8 fusion.84
  925.7 1.6 convolution_add_fusion
  (191 shorter events, 46.7 us)
Async XLA Ops:
  7.2 27.3 %copy-start = (bf16[1024,128]{1,0:T(8,128)(2,1)S(1)}, bf16[1024,128]{1,0:T(8,128)(2,1)}, u32[]{:S(2)}) copy-start(bf16[1024,128]{1,0:T(8,128)(2,1)} %param.39) | copy-start | bytes 786436
  34.5 3.1 copy-start.1
  48.1 6.0 copy-start.26
  48.1 6.2 copy-start.27
  48.1 6.4 copy-start.25
  48.1 191.7 %all-to-all-start.1 = ((bf16[64,2,2,128,128]{4,3,1,2,0:T(8,128)(2,1)}), bf16[64,2,2,128,128]{4,3,1,2,0:T(8,128)(2,1)}, u32[]{:S(2)}, u32[]{:S(2)}) async-start(bf16[64,2,2,128,128]{4,3,1,2,0:T(8,128)(2,1)} %pad_maximum_fusion), calls=%async_computation.1 | async-start | bytes 16777216 | tf_op jit(solution)/shard_map/all_to_all | solution.py:173
  250.2 7.3 copy-start.24
  259.1 2.0 copy-start.7
  259.5 2.1 copy-start.9
  260.7 1.4 copy-start.11
  293.5 12.5 %copy-start.29 = (s32[2]{0:T(128)S(1)}, s32[2]{0:T(128)}, u32[]{:S(2)}) copy-start(s32[2]{0:T(128)} %param.45) | copy-start | bytes 28
  293.5 613.2 %all-to-all-start.2 = ((bf16[64,2,2,128,128]{4,3,2,1,0:T(8,128)(2,1)}), bf16[64,2,2,128,128]{4,3,2,1,0:T(8,128)(2,1)}, u32[]{:S(2)}, u32[]{:S(2)}) async-start(bf16[64,2,2,128,128]{4,3,2,1,0:T(8,128)(2,1)} %bitcast.283), calls=%async_computation.2 | async-start | bytes 16777216 | tf_op jit(solution)/shard_map/all_to_all | solution.py:199
  299.8 595.6 %all-reduce.5.cloned.1.call-start = ((), (), s32[]{:S(2)}) async-start(), calls=%async_computation.3 | async-start | bytes 524288 | tf_op jit(solution)/shard_map/psum | solution.py:150
  300.5 437.4 %collective-permute-start = (bf16[2,128,128]{2,1,0:T(8,128)(2,1)}, bf16[2,128,128]{2,1,0:T(8,128)(2,1)}, u32[]{:S(2)}, u32[]{:S(2)}) collective-permute-start(bf16[2,128,128]{2,1,0:T(8,128)(2,1)} %get-tuple-element.192), channel_id=1, source_target_pairs={{0,4},{4,8},{8,12},{12,16},{16,20},{20,24},{24,28},{28,32},{32,36}... | collective-permute-start | bytes 196616 | tf_op jit(solution)/shard_map/ppermute | solution.py:18
  304.1 433.8 %collective-permute-start.1 = (bf16[2,128,128]{2,1,0:T(8,128)(2,1)}, bf16[2,128,128]{2,1,0:T(8,128)(2,1)}, u32[]{:S(2)}, u32[]{:S(2)}) collective-permute-start(bf16[2,128,128]{2,1,0:T(8,128)(2,1)} %get-tuple-element.193), channel_id=1, source_target_pairs={{4,0},{8,4},{12,8},{16,12},{20,16},{24,20},{28,24},{32,28},{36,32}... | collective-permute-start | bytes 196616 | tf_op jit(solution)/shard_map/ppermute | solution.py:19
  719.5 9.4 copy-start.28
  728.9 5.6 copy-start.21
  739.6 3.2 copy-start.23
  745.0 1.2 copy-start.4
  745.8 1.2 copy-start.6
  746.2 1.1 copy-start.20
  748.2 11.3 %collective-permute-start.2 = (bf16[2,128,128]{1,2,0:T(8,128)(2,1)S(1)}, bf16[2,128,128]{1,2,0:T(8,128)(2,1)S(1)}, u32[]{:S(2)}, u32[]{:S(2)}) collective-permute-start(bf16[2,128,128]{1,2,0:T(8,128)(2,1)S(1)} %get-tuple-element.201), channel_id=1, source_target_pairs={{0,4},{4,8},{8,12},{12,16},{16,20},{20,24},{24,28},{28,32},{32,36}... | collective-permute-start | bytes 196616 | tf_op jit(solution)/shard_map/ppermute | solution.py:18
  751.9 152.2 %copy-start.8 = (bf16[8,2,128,128]{3,2,1,0:T(8,128)(2,1)S(1)}, bf16[8,2,128,128]{3,2,1,0:T(8,128)(2,1)}, u32[]{:S(2)}) copy-start(bf16[8,2,128,128]{3,2,1,0:T(8,128)(2,1)} %copy-done.7) | copy-start | bytes 1572868
  751.9 7.7 collective-permute-start.3
  758.7 145.7 %copy-start.10 = (bf16[8,2,128,128]{3,2,1,0:T(8,128)(2,1)S(1)}, bf16[8,2,128,128]{3,2,1,0:T(8,128)(2,1)}, u32[]{:S(2)}) copy-start(bf16[8,2,128,128]{3,2,1,0:T(8,128)(2,1)} %copy-done.9) | copy-start | bytes 1572868
  895.4 9.2 copy-start.12
  895.4 9.5 %copy-start.15 = (f32[8,128,2,64]{1,3,2,0:T(8,128)S(1)}, f32[8,128,2,64]{1,3,2,0:T(8,128)}, u32[]{:S(2)}) copy-start(f32[8,128,2,64]{1,3,2,0:T(8,128)} %convolution_bitcast_fusion.9) | copy-start | bytes 1572868
  895.4 9.5 %copy-start.16 = (f32[8,128,2,64]{1,3,2,0:T(8,128)S(1)}, f32[8,128,2,64]{1,3,2,0:T(8,128)}, u32[]{:S(2)}) copy-start(f32[8,128,2,64]{1,3,2,0:T(8,128)} %convolution_bitcast_fusion.10) | copy-start | bytes 1572868
  895.4 9.5 %copy-start.17 = (f32[8,128,2,64]{1,3,2,0:T(8,128)S(1)}, f32[8,128,2,64]{1,3,2,0:T(8,128)}, u32[]{:S(2)}) copy-start(f32[8,128,2,64]{1,3,2,0:T(8,128)} %convolution_bitcast_fusion.12) | copy-start | bytes 1572868
  895.4 9.5 %copy-start.18 = (f32[8,128,2,64]{1,3,2,0:T(8,128)S(1)}, f32[8,128,2,64]{1,3,2,0:T(8,128)}, u32[]{:S(2)}) copy-start(f32[8,128,2,64]{1,3,2,0:T(8,128)} %convolution_bitcast_fusion.11) | copy-start | bytes 1572868
  920.0 5.8 copy-start.2
  927.3 3.0 copy-start.14
  (5 other events, 4.6 us)
Sparse Core Ops, SparseCore 0:
  721.3 174.1 all-reduce.4
where the time goes:
time: 940 us; the launch traced here: 939 us
  blocking collectives  432 us (46%)
  waiting for transfers between devices  318 us (34%)
  local copies, waits for them, and re-layouts  81.9 us (9%)
  other arithmetic  35.4 us (4%)
  starting transfers between devices  27 us (3%)
  matrix products  25.8 us (3%)
  between operations  18.7 us (2%)
    psum x1, blocking collectives, shards(): shared = lax.psum(own_part, 'seq').astype(jnp.bfloat16)  409 us
    all_to_all x1, waiting for transfers between devices, shards(): lax.all_to_all(outgoing.reshape(owners, capacity, 2, BLOCK, features), 's...  185 us
    psum x1, waiting for transfers between devices, shards(): totals = lax.psum(jnp.stack(global_pieces), 'seq')  133 us
    all_to_all x1, blocking collectives, shards(): lax.all_to_all(requested.reshape(owners, capacity), 'seq', split_axis=0,...  22.2 us
  transfers between devices with their start and end apart: 7, of which 2 were waited for; matrix products, arithmetic and copies ran while one was open for 5% of the time, Pallas kernels for 0%

commit v1 on v0

v1 whole, which is shorter than its diff:
```python
import functools
import math

import jax
import jax.numpy as jnp
from jax import lax
from jax.experimental import pallas as pl
from jax.experimental.pallas import tpu as pltpu
from jax.sharding import PartitionSpec as P

BLOCK = 128
NY, NZ, NC = 4, 8, 2
MESH = pl.DeviceIdType.MESH
F32 = jnp.float32
BF16 = jnp.bfloat16


def place():
    seq = lax.axis_index("seq")
    core = lax.rem(seq, NC)
    z = lax.rem(seq // NC, NZ)
    y = seq // (NC * NZ)
    return y, z, core


def device(y, z, core):
    return {"seq": (y * NZ + z) * NC + core}


def side_kernel(out_ref, grad_ref, norm_ref, owner_ref, local_ref, nd_ref, refs_ref):
    blocks = nd_ref.shape[0]
    for b in range(blocks):
        rows = pl.ds(b * BLOCK, BLOCK)
        product = out_ref[rows, :].astype(F32) * grad_ref[rows, :].astype(F32)
        turned = product.T
        half = turned.shape[0] // 2
        nd_ref[b, 0:2, :] = norm_ref[:, rows]
        nd_ref[b, 2:3, :] = jnp.sum(turned[:half], axis=0, keepdims=True)
        nd_ref[b, 3:4, :] = jnp.sum(turned[half:], axis=0, keepdims=True)
        nd_ref[b, 4:8, :] = jnp.zeros((4, BLOCK), F32)
    refs_ref[...] = jnp.zeros(refs_ref.shape, jnp.int32)
    refs_ref[:, 0:3] = owner_ref[...] * blocks + local_ref[...]


def gather_kernel(
    q_ref, d_ref, k_ref, v_ref, nd_ref, rf_ref,
    qd_out, kv_out, nd_out, rf_out,
    zsend, zrecv, ysend, yrecv, csend, crecv, lsem,
):
    y, z, c = place()
    zdev = [device(y, lax.rem(z + 1, NZ), c), device(y, lax.rem(z + NZ - 1, NZ), c)]
    ydev = [device(lax.rem(y + 1, NY), z, c), device(lax.rem(y + NY - 1, NY), z, c)]
    cdev = device(y, z, 1 - c)

    barrier = pltpu.get_barrier_semaphore()
    for target in zdev + ydev + [cdev]:
        pl.semaphore_signal(barrier, inc=1, device_id=target, device_id_type=MESH)
    pl.semaphore_wait(barrier, 5)

    own = [q_ref, d_ref, nd_ref, rf_ref]

    def zslot(part, slot):
        if part < 2:
            return qd_out.at[slot, part]
        return (nd_out, rf_out)[part - 2].at[slot]

    def zcopy(way, step, part):
        slot = lax.rem(z + (NZ - step + 1 if way == 0 else step - 1), NZ)
        return pltpu.make_async_remote_copy(
            src_ref=own[part] if step == 1 else zslot(part, slot),
            dst_ref=zslot(part, slot),
            send_sem=zsend.at[way, step - 1, part],
            recv_sem=zrecv.at[way, step - 1, part],
            device_id=zdev[way],
            device_id_type=MESH,
        )

    def zparts(way, step):
        if step < 4:
            return (2, 3, 0, 1)
        return (2, 3, 0) if way == 0 else (1,)

    def ycopy(way, step, part):
        row = lax.rem(y + ((NY if step == 1 else NY - 1) if way == 0 else step - 1), NY)
        slot = row * NC + c
        return pltpu.make_async_remote_copy(
            src_ref=(k_ref, v_ref)[part] if step == 1 else kv_out.at[slot, part],
            dst_ref=kv_out.at[slot, part],
            send_sem=ysend.at[way, step - 1, part],
            recv_sem=yrecv.at[way, step - 1, part],
            device_id=ydev[way],
            device_id_type=MESH,
        )

    def ccopy(offset, part):
        slot = lax.rem(y + offset, NY) * NC + c
        return pltpu.make_async_remote_copy(
            src_ref=(k_ref, v_ref)[part] if offset == 0 else kv_out.at[slot, part],
            dst_ref=kv_out.at[slot, part],
            send_sem=csend.at[offset, part],
            recv_sem=crecv.at[offset, part],
            device_id=cdev,
            device_id_type=MESH,
        )

    for part in (2, 3, 0, 1):
        for way in (0, 1):
            zcopy(way, 1, part).start()
    for part in (0, 1):
        for way in (0, 1):
            ycopy(way, 1, part).start()
        ccopy(0, part).start()
    local = [
        pltpu.make_async_copy(q_ref, qd_out.at[z, 0], lsem.at[0]),
        pltpu.make_async_copy(d_ref, qd_out.at[z, 1], lsem.at[1]),
        pltpu.make_async_copy(nd_ref, nd_out.at[z], lsem.at[2]),
        pltpu.make_async_copy(rf_ref, rf_out.at[z], lsem.at[3]),
        pltpu.make_async_copy(k_ref, kv_out.at[y * NC + c, 0], lsem.at[4]),
        pltpu.make_async_copy(v_ref, kv_out.at[y * NC + c, 1], lsem.at[5]),
    ]
    for copy in local:
        copy.start()

    def zround(step):
        for part in (2, 3, 0, 1):
            for way in (0, 1):
                if part in zparts(way, step):
                    zcopy(way, step, part).wait_recv()
                    if step < 4 and part in zparts(way, step + 1):
                        zcopy(way, step + 1, part).start()

    zround(1)
    for part in (0, 1):
        for way in (0, 1):
            ycopy(way, 1, part).wait_recv()
            if part == way:
                ycopy(way, 2, part).start()
            ccopy(NY - 1 if way == 0 else 1, part).start()
    zround(2)
    for way in (0, 1):
        ycopy(way, 2, way).wait_recv()
        ccopy(2, way).start()
    zround(3)
    zround(4)
    for offset in range(NY):
        for part in (0, 1):
            ccopy(offset, part).wait()
    for way in (0, 1):
        for step in range(1, 5):
            for part in zparts(way, step):
                zcopy(way, step, part).wait_send()
        for part in (0, 1):
            ycopy(way, 1, part).wait_send()
        ycopy(way, 2, way).wait_send()
    for copy in local:
        copy.wait()


def pair_terms(q, d, nd, k, v, factor):
    lane = lax.broadcasted_iota(jnp.int32, k.shape, 1)
    half = k.shape[1] // 2
    zero = jnp.zeros_like(k)
    k2 = jnp.concatenate([jnp.where(lane < half, k, zero), jnp.where(lane < half, zero, k)], axis=0)
    v2 = jnp.concatenate([jnp.where(lane < half, v, zero), jnp.where(lane < half, zero, v)], axis=0)
    across = (((1,), (1,)), ((), ()))
    scores = lax.dot_general(k2, q, across, preferred_element_type=F32)
    grads = lax.dot_general(v2, d, across, preferred_element_type=F32)
    rows = k.shape[0]

    def per_head(first):
        return jnp.concatenate(
            [jnp.broadcast_to(nd[i : i + 1, :], (rows, BLOCK)) for i in (first, first + 1)], axis=0
        )

    weights = jnp.exp(scores * factor - per_head(0))
    grad_scores = weights * (grads - per_head(2))
    weights_low = weights.astype(BF16)
    scores_low = grad_scores.astype(BF16)
    dv2 = jnp.dot(weights_low, d, preferred_element_type=F32)
    dk2 = jnp.dot(scores_low, q, preferred_element_type=F32)
    dq = lax.dot_general(scores_low, k2, (((0,), (0,)), ((), ())), preferred_element_type=F32)
    dv = jnp.where(lane < half, dv2[:rows], dv2[rows:])
    dk = jnp.where(lane < half, dk2[:rows], dk2[rows:])
    return dq * factor, dk * factor, dv


def pair_kernel(
    glob_ref, rf_ref, qd_ref, kv_ref, nd_ref, dq_out, dkv_out, dq_acc, dk_acc, dv_acc, list_ref, *, factor
):
    y, z, c = place()
    blocks = nd_ref.shape[1]
    chunk = 8

    @pl.loop(0, NZ * blocks)
    def _(i):
        zero = jnp.zeros((BLOCK, BLOCK), F32)
        dq_acc[i] = zero
        dk_acc[i] = zero
        dv_acc[i] = zero

    def key_place(key):
        owner = key // blocks
        here = lax.rem(owner // NC, NZ) == z
        slot = (owner // (NC * NZ)) * NC + lax.rem(owner, NC)
        return here, slot * blocks + lax.rem(key, blocks)

    def add(n, query, key, wanted):
        here, where = key_place(key)
        list_ref[n] = query * (NZ * blocks) + where
        return n + jnp.where(jnp.logical_and(here, wanted), 1, 0).astype(jnp.int32)

    last = NY * NZ * NC * blocks - 1

    def per_query(i, n):
        slot = i // blocks
        b = lax.rem(i, blocks)
        for r in range(3):
            n = add(n, i, rf_ref[slot, b, r], True)
        block = ((y * NZ + slot) * NC + c) * blocks + b
        for key in (block - 1, block, block + 1):
            n = add(n, i, jnp.clip(key, 0, last), jnp.logical_and(key >= 0, key <= last))
        for g in range(2):
            n = add(n, i, glob_ref[g], True)
        return n

    count = lax.fori_loop(0, NZ * blocks, per_query, jnp.int32(0))

    @pl.loop(0, count)
    def _(i):
        item = list_ref[i]
        query = item // (NZ * blocks)
        key = lax.rem(item, NZ * blocks)
        qs = query // blocks
        qb = lax.rem(query, blocks)
        qrows = pl.ds(pl.multiple_of(qb * BLOCK, BLOCK), BLOCK)
        ks = key // blocks
        krows = pl.ds(pl.multiple_of(lax.rem(key, blocks) * BLOCK, BLOCK), BLOCK)
        dq, dk, dv = pair_terms(
            qd_ref[qs, 0, qrows, :],
            qd_ref[qs, 1, qrows, :],
            nd_ref[qs, qb],
            kv_ref[ks, 0, krows, :],
            kv_ref[ks, 1, krows, :],
            factor,
        )
        dq_acc[query] += dq
        dk_acc[key] += dk
        dv_acc[key] += dv

    @pl.loop(0, NZ * blocks)
    def _(i):
        slot = i // blocks
        rows = pl.ds(pl.multiple_of(lax.rem(i, blocks) * BLOCK, BLOCK), BLOCK)
        dq_out[slot, rows, :] = dq_acc[i].astype(BF16)
        dkv_out[slot, 0, rows, :] = dk_acc[i].astype(BF16)
        dkv_out[slot, 1, rows, :] = dv_acc[i].astype(BF16)


def reduce_kernel(
    dq_in, dkv_in, dq_out, dk_out, dv_out,
    zbuf, zin, cin, csum, ybuf, yin,
    zsend, zrecv, ysend, yrecv, csend, crecv,
):
    y, z, c = place()
    half = dq_out.shape[0] // 2
    zdev = [device(y, lax.rem(z + 1, NZ), c), device(y, lax.rem(z + NZ - 1, NZ), c)]
    ydev = [device(lax.rem(y + 1, NY), z, c), device(lax.rem(y + NY - 1, NY), z, c)]
    cdev = device(y, z, 1 - c)

    barrier = pltpu.get_barrier_semaphore()
    for target in zdev + ydev + [cdev]:
        pl.semaphore_signal(barrier, inc=1, device_id=target, device_id_type=MESH)
    pl.semaphore_wait(barrier, 5)

    def zparts(way, step):
        return (way,) if step == 1 else (0, 1)

    def zplain(way, step, part):
        return step == 1 or (step == 2 and part != way)

    def ztarget(way, step):
        return lax.rem(z + (5 - step if way == 0 else NZ - 5 + step), NZ)

    def zcopy(way, step, part):
        rows = pl.ds(part * half, half)
        if zplain(way, step, part):
            source = dq_in.at[ztarget(way, step), rows]
        else:
            source = zbuf.at[way, step - 1, rows]
        return pltpu.make_async_remote_copy(
            src_ref=source,
            dst_ref=zin.at[way, step - 1, rows],
            send_sem=zsend.at[way, step - 1, part],
            recv_sem=zrecv.at[way, step - 1, part],
            device_id=zdev[way],
            device_id_type=MESH,
        )

    def ccopy(offset, part):
        row = lax.rem(y + offset, NY)
        return pltpu.make_async_remote_copy(
            src_ref=dkv_in.at[row * NC + 1 - c, part],
            dst_ref=cin.at[offset, part],
            send_sem=csend.at[offset, part],
            recv_sem=crecv.at[offset, part],
            device_id=cdev,
            device_id_type=MESH,
        )

    def ycopy(way, step, part):
        return pltpu.make_async_remote_copy(
            src_ref=csum.at[2, part] if step == 1 else ybuf.at[way, part],
            dst_ref=yin.at[way, step - 1, part],
            send_sem=ysend.at[way, step - 1, part],
            recv_sem=yrecv.at[way, step - 1, part],
            device_id=ydev[way],
            device_id_type=MESH,
        )

    for offset in (2, 1, 3, 0):
        for part in (0, 1):
            ccopy(offset, part).start()
    for way in (0, 1):
        zcopy(way, 1, way).start()
        zcopy(way, 2, 1 - way).start()

    def zround(step):
        for part in (0, 1):
            for way in (0, 1):
                if part in zparts(way, step):
                    zcopy(way, step, part).wait_recv()
                    rows = pl.ds(part * half, half)
                    mine = dq_in[ztarget(way, step + 1), rows, :].astype(F32)
                    zbuf[way, step, rows, :] = (mine + zin[way, step - 1, rows, :].astype(F32)).astype(BF16)
                    zcopy(way, step + 1, part).start()

    def cadd(offset, part):
        ccopy(offset, part).wait_recv()
        row = lax.rem(y + offset, NY)
        mine = dkv_in[row * NC + c, part].astype(F32)
        return mine + cin[offset, part].astype(F32)

    for part in (0, 1):
        csum[2, part] = cadd(2, part).astype(BF16)
        ycopy(part, 1, part).start()
    zround(1)
    for way in (0, 1):
        offset = 1 if way == 0 else NY - 1
        for part in (1 - way, way):
            total = cadd(offset, part)
            if part == way:
                ycopy(way, 1, part).wait_recv()
                total = total + yin[way, 0, part].astype(F32)
            ybuf[way, part] = total.astype(BF16)
            ycopy(way, 2, part).start()
    zround(2)
    zround(3)
    for part, out in ((0, dk_out), (1, dv_out)):
        total = cadd(0, part)
        for way in (0, 1):
            ycopy(way, 2, part).wait_recv()
            total = total + yin[way, 1, part].astype(F32)
        out[...] = total.astype(BF16)
    for part in (0, 1):
        rows = pl.ds(part * half, half)
        total = dq_in[z, rows, :].astype(F32)
        for way in (0, 1):
            zcopy(way, 4, part).wait_recv()
            total = total + zin[way, 3, rows, :].astype(F32)
        dq_out[rows, :] = total.astype(BF16)
    for way in (0, 1):
        for step in range(1, 5):
            for part in zparts(way, step):
                zcopy(way, step, part).wait_send()
        ycopy(way, 1, way).wait_send()
        for part in (0, 1):
            ycopy(way, 2, part).wait_send()
    for offset in range(NY):
        for part in (0, 1):
            ccopy(offset, part).wait_send()


def shards(queries, keys, values, outputs, d_outputs, log_norm, rand_owner, rand_local, glob_blocks):
    tokens, features = queries.shape
    blocks = tokens // BLOCK
    factor = 1.0 / math.sqrt(features // log_norm.shape[0])
    vmem = pl.BlockSpec(memory_space=pltpu.VMEM)
    smem = pl.BlockSpec(memory_space=pltpu.SMEM)
    anywhere = pl.BlockSpec(memory_space=pl.ANY)
    dma = pltpu.SemaphoreType.DMA

    side, refs = pl.pallas_call(
        side_kernel,
        out_shape=(
            jax.ShapeDtypeStruct((blocks, 8, BLOCK), F32),
            jax.ShapeDtypeStruct((blocks, BLOCK), jnp.int32),
        ),
        in_specs=[vmem] * 5,
        out_specs=(vmem, vmem),
        name="side",
    )(outputs, d_outputs, log_norm, rand_owner, rand_local)

    qd, kv, nd, rf = pl.pallas_call(
        gather_kernel,
        out_shape=(
            jax.ShapeDtypeStruct((NZ, 2, tokens, features), BF16),
            jax.ShapeDtypeStruct((NY * NC, 2, tokens, features), BF16),
            jax.ShapeDtypeStruct((NZ, blocks, 8, BLOCK), F32),
            jax.ShapeDtypeStruct((NZ, blocks, BLOCK), jnp.int32),
        ),
        in_specs=[vmem] * 6,
        out_specs=(anywhere,) * 4,
        scratch_shapes=[
            dma((2, 4, 4)), dma((2, 4, 4)), dma((2, 2, 2)), dma((2, 2, 2)),
            dma((NY, 2)), dma((NY, 2)), dma((6,)),
        ],
        compiler_params=pltpu.CompilerParams(collective_id=0, has_side_effects=True),
        name="gather",
    )(queries, d_outputs, keys, values, side, refs)

    dq_part, dkv_part = pl.pallas_call(
        functools.partial(pair_kernel, factor=factor),
        out_shape=(
            jax.ShapeDtypeStruct((NZ, tokens, features), BF16),
            jax.ShapeDtypeStruct((NY * NC, 2, tokens, features), BF16),
        ),
        in_specs=[smem, smem, vmem, vmem, vmem],
        out_specs=(vmem, vmem),
        scratch_shapes=[
            pltpu.VMEM((NZ * blocks, BLOCK, features), F32),
            pltpu.VMEM((NY * NC * blocks, BLOCK, features), F32),
            pltpu.VMEM((NY * NC * blocks, BLOCK, features), F32),
            pltpu.SMEM((NZ * blocks * 8 + 8,), jnp.int32),
        ],
        compiler_params=pltpu.CompilerParams(vmem_limit_bytes=50 * 1024 * 1024),
        name="pairs",
    )(glob_blocks, rf, qd, kv, nd)

    return tuple(pl.pallas_call(
        reduce_kernel,
        out_shape=(jax.ShapeDtypeStruct((tokens, features), BF16),) * 3,
        in_specs=[vmem] * 2,
        out_specs=(vmem,) * 3,
        scratch_shapes=[
            pltpu.VMEM((2, 4, tokens, features), BF16),
            pltpu.VMEM((2, 4, tokens, features), BF16),
            pltpu.VMEM((NY, 2, tokens, features), BF16),
            pltpu.VMEM((NY, 2, tokens, features), BF16),
            pltpu.VMEM((2, 2, tokens, features), BF16),
            pltpu.VMEM((2, 2, 2, tokens, features), BF16),
            dma((2, 4, 2)), dma((2, 4, 2)), dma((2, 2, 2)), dma((2, 2, 2)), dma((NY, 2)), dma((NY, 2)),
        ],
        compiler_params=pltpu.CompilerParams(
            collective_id=1, has_side_effects=True, vmem_limit_bytes=50 * 1024 * 1024
        ),
        name="reduce",
    )(dq_part, dkv_part))


def solution(mesh):
    placed = (
        P("seq", "head"), P("seq", "head"), P("seq", "head"), P("seq", "head"), P("seq", "head"),
        P("head", "seq"), P("seq", None), P("seq", None), P(),
    )
    return jax.shard_map(
        shards,
        mesh=mesh,
        in_specs=placed,
        out_specs=(P("seq", "head"), P("seq", "head"), P("seq", "head")),
        check_vma=False,
    )
```

time: 940 us -> 152 us (0.16)
  blocking collectives: 432 us -> 0 us
  waiting for transfers between devices: 318 us -> 0 us
  Pallas kernels: 0 us -> 144 us
  local copies, waits for them, and re-layouts: 81.9 us -> 7.16 us
  other arithmetic: 35.4 us -> 0 us
  starting transfers between devices: 27 us -> 0 us
  matrix products: 25.8 us -> 0 us
  between operations: 18.7 us -> 0.66 us
    psum x1 -> x0, blocking collectives: 409 us -> none  [shards(): shared = lax.psum(own_part, 'seq').astype(jnp.bfloat16)]
    all_to_all x2 -> x0, waiting for transfers between devices: 185 us -> none  [the longest x1 185 us: shards(): lax.all_to_all(outgoing.reshape(owners, capacity, 2, BLOCK, features), 's...]
    pallas_call x0 -> x4, Pallas kernels: none -> 144 us  [the longest x1 54 us: shards(): pl.pallas_call(gather_kernel, out_shape=(jax.ShapeDtypeStruct((NZ, 2, tok...]
    psum x1 -> x0, waiting for transfers between devices: 133 us -> none  [shards(): totals = lax.psum(jnp.stack(global_pieces), 'seq')]
    dot_general x42 -> x0, matrix products: 25.8 us -> none  [the longest x8 6.7 us: pair_terms(): jnp.einsum('nhqk,nkhd->nqhd', scores_low, key_rows, preferred_element_typ...]
    all_to_all x1 -> x0, blocking collectives: 22.2 us -> none  [shards(): lax.all_to_all(requested.reshape(owners, capacity), 'seq', split_axis=0,...]
    another operation x2 -> x0, local copies, waits for them, and re-layouts: 15.2 us -> none  [the longest x1 13.3 us: add_by_block(): flat_terms = targets.reshape(targets.shape[0], -1)]
    ppermute x4 -> x0, starting transfers between devices: 14.7 us -> none  [the longest x2 7.56 us: extended(): after = lax.ppermute(leading, axis, down)]
  transfers between devices with their start and end apart: 7 -> 0, of which waited for: 2 -> 0; matrix products, arithmetic and copies ran while one was open for 5% -> 0% of each run, Pallas kernels for 0% -> 0%
where the time goes in v1:
time: 152 us
  Pallas kernels  144 us (95%)
  local copies, waits for them, and re-layouts  7.16 us (5%)
    pallas_call x1, Pallas kernels, shards(): pl.pallas_call(gather_kernel, out_shape=(jax.ShapeDtypeStruct((NZ, 2, tok...  54 us
    pallas_call x1, Pallas kernels, shards(): pl.pallas_call(reduce_kernel, out_shape=(jax.ShapeDtypeStruct((tokens, fe...  47.7 us
    pallas_call x1, Pallas kernels, shards(): pl.pallas_call(functools.partial(pair_kernel, factor=factor), out_shape=(...  40.4 us
    unnamed x11, local copies, waits for them, and re-layouts  7.16 us

profile of v1, /device:TPU:1, one launch (start us, length us, event | category | flops | bytes accessed | tf_op | source)
XLA Modules:
  0.0 151.8 jit_solution(1264872885227445887)
XLA Ops:
  0.6 1.3 copy.12.owner_ref
  2.0 1.3 copy.13.local_ref
  3.3 1.9 %side.1 = (f32[8,8,128]{2,1,0:T(8,128)}, s32[8,128]{1,0:T(8,128)}) custom-call(bf16[1024,128]{1,0:T(8,128)(2,1)} %out_ref.1, bf16[1024,128]{1,0:T(8,128)(2,1)} %d_ref.1, f32[2,1024]{1,0:T(2,128)} %norm_ref.1, s32[8,3]{1,0:T(8,128)} %copy.12.owner_ref, s32[8,3]{1,0:T(8,128)} %copy.13.local_ref), custom_call_target="tpu_custom_call" | custom-call | tf_op jit(solution)/shard_map/side/pallas_call | solution.py:392
  5.2 54.0 %gather.1 = (bf16[8,2,1024,128]{3,2,1,0:T(8,128)(2,1)}, bf16[8,2,1024,128]{3,2,1,0:T(8,128)(2,1)}, f32[8,8,8,128]{3,2,1,0:T(8,128)}, s32[8,8,128]{2,1,0:T(8,128)}) custom-call(bf16[1024,128]{1,0:T(8,128)(2,1)} %q_ref.1, bf16[1024,128]{1,0:T(8,128)(2,1)} %d_ref.1, bf16[1024,128]{1,0:T(8,128)(2,1)} %k_ref.1, bf16[1024,128]{1,0:T(8,128)(2,1)} %v_ref.1, ...), custom_call_target="tpu_custom_call" | custom-call | tf_op jit(solution)/shard_map/gather/pallas_call | solution.py:403
  59.2 0.0 copy-start
  59.2 0.9 copy-done
  60.2 0.0 copy-start.1
  60.2 0.8 copy-done.1
  60.9 0.0 copy-start.2
  60.9 0.7 copy-done.2
  61.6 40.4 %pairs.1 = (bf16[8,1024,128]{2,1,0:T(8,128)(2,1)S(1)}, bf16[8,2,1024,128]{3,2,1,0:T(8,128)(2,1)}) custom-call(s32[2]{0:T(128)S(1)} %copy-done.2, s32[8,8,128]{2,1,0:T(8,128)S(1)} %copy-done.1, bf16[8,2,1024,128]{3,2,1,0:T(8,128)(2,1)} %get-tuple-element.14.qd_ref, bf16[8,2,1024,128]{3,2,1,0:T(8,128)(2,1)} %get-tuple-element.15.kv_ref, ...), custom_call_target="tpu_custom_call" | custom-call | tf_op jit(solution)/shard_map/pairs/pallas_call | solution.py:421
  102.0 47.7 %reduce.1 = (bf16[1024,128]{1,0:T(8,128)(2,1)S(1)}, bf16[1024,128]{1,0:T(8,128)(2,1)S(1)}, bf16[1024,128]{1,0:T(8,128)(2,1)S(1)}) custom-call(bf16[8,1024,128]{2,1,0:T(8,128)(2,1)S(1)} %get-tuple-element.17.dq_in, bf16[8,2,1024,128]{3,2,1,0:T(8,128)(2,1)} %get-tuple-element.18.dkv_in), custom_call_target="tpu_custom_call" | custom-call | tf_op jit(solution)/shard_map/reduce/pallas_call | solution.py:439
  149.7 0.7 copy.17
  150.4 0.7 copy.18
  151.1 0.7 copy.19
Async XLA Ops:
  59.2 1.0 copy-start
  60.2 0.8 copy-start.1
  60.9 0.7 copy-start.2

commit v2 on v1

v2 whole, which is shorter than its diff:
```python
import functools
import math

import jax
import jax.numpy as jnp
from jax import lax
from jax.experimental import pallas as pl
from jax.experimental.pallas import tpu as pltpu
from jax.sharding import PartitionSpec as P

BLOCK = 128
NY, NZ, NC = 4, 8, 2
MESH = pl.DeviceIdType.MESH
F32 = jnp.float32
BF16 = jnp.bfloat16
MIB = 1024 * 1024


def place():
    seq = lax.axis_index("seq")
    core = lax.rem(seq, NC)
    z = lax.rem(seq // NC, NZ)
    y = seq // (NC * NZ)
    return y, z, core


def device(y, z, core):
    return {"seq": (y * NZ + z) * NC + core}


def side_kernel(
    out_ref, grad_ref, norm_ref, owner_ref, local_ref, key_ref, value_ref, glob_ref, nd_ref, refs_ref, cand_ref
):
    blocks = out_ref.shape[0] // BLOCK
    for b in range(blocks):
        rows = pl.ds(b * BLOCK, BLOCK)
        product = out_ref[rows, :].astype(F32) * grad_ref[rows, :].astype(F32)
        turned = product.T
        half = turned.shape[0] // 2
        first = 4 * (b % 2)
        nd_ref[b // 2, first : first + 2, :] = norm_ref[:, rows]
        nd_ref[b // 2, first + 2 : first + 3, :] = jnp.sum(turned[:half], axis=0, keepdims=True)
        nd_ref[b // 2, first + 3 : first + 4, :] = jnp.sum(turned[half:], axis=0, keepdims=True)
    owner = owner_ref[...]
    column = jnp.bitwise_and(owner >> 1, NZ - 1)
    member = (owner >> 4) * NC + jnp.bitwise_and(owner, 1)
    refs_ref[...] = jnp.zeros(refs_ref.shape, jnp.int32)
    refs_ref[0:3, 0:blocks] = (column * (NY * NC) + member) * blocks + local_ref[...]
    seq = lax.axis_index("seq")
    half = BLOCK // 2
    for g in range(2):
        where = glob_ref[g]
        mine = (where // blocks) == seq
        start = pl.multiple_of(lax.rem(where, blocks) * BLOCK, BLOCK)
        for i, ref in enumerate((key_ref, value_ref)):
            block = ref[pl.ds(start, BLOCK), :]
            block = jnp.where(mine, block, jnp.zeros_like(block))
            cand_ref[4 * g + 2 * i] = block[:half]
            cand_ref[4 * g + 2 * i + 1] = block[half:]


def pair_terms(q, d, nd, k, v, factor):
    lane = lax.broadcasted_iota(jnp.int32, k.shape, 1)
    half = k.shape[1] // 2
    rows = k.shape[0]
    zero = jnp.zeros_like(k)
    k = k * factor
    k2 = jnp.concatenate([jnp.where(lane < half, k, zero), jnp.where(lane < half, zero, k)], axis=0)
    v2 = jnp.concatenate([jnp.where(lane < half, v, zero), jnp.where(lane < half, zero, v)], axis=0)
    across = (((1,), (1,)), ((), ()))
    scores = lax.dot_general(k2, q, across, preferred_element_type=F32)
    grads = lax.dot_general(v2, d, across, preferred_element_type=F32)

    def per_head(first):
        return jnp.concatenate(
            [jnp.broadcast_to(nd[i : i + 1, :], (rows, BLOCK)) for i in (first, first + 1)], axis=0
        )

    weights = jnp.exp(scores - per_head(0))
    grad_scores = weights * (grads - per_head(2))
    weights_low = weights.astype(BF16)
    scores_low = grad_scores.astype(BF16)
    dv2 = jnp.dot(weights_low, d, preferred_element_type=F32)
    dk2 = jnp.dot(scores_low, q, preferred_element_type=F32)
    dq = lax.dot_general(scores_low, k2, (((0,), (0,)), ((), ())), preferred_element_type=F32)
    dv = jnp.where(lane < half, dv2[:rows], dv2[rows:])
    dk = jnp.where(lane < half, dk2[:rows], dk2[rows:])
    return dq, dk, dv


def query_rows(nd_tile, b):
    return jnp.where(lax.rem(b, 2) == 0, nd_tile[0:4], nd_tile[4:8])


def gather_kernel(
    q_ref, d_ref, k_ref, v_ref, nd_ref, rf_ref, cand_ref,
    qd_out, kv_out, nd_out, rf_out, dq_out, dk_out, dv_out, total_out,
    g1in, s1, g2in, s2, g3in, s3, gkv, gacc, r1in, t1, r2in, t2, r3in,
    zsend, zrecv, ysend, yrecv, csend, crecv, gsend, grecv, lsem,
    *, factor,
):
    y, z, c = place()
    blocks = q_ref.shape[0] // BLOCK
    half = BLOCK // 2
    zdev = [device(y, lax.rem(z + 1, NZ), c), device(y, lax.rem(z + NZ - 1, NZ), c)]
    ydev = [device(lax.rem(y + 1, NY), z, c), device(lax.rem(y + NY - 1, NY), z, c)]
    cdev = device(y, z, 1 - c)
    me = y * NC + c

    def member(offset):
        return lax.rem(me + offset, NY * NC)

    def member_device(offset):
        other = member(offset)
        return device(other // NC, z, lax.rem(other, NC))

    def row_device(offset):
        return device(y, lax.rem(z + offset, NZ), c)

    barrier = pltpu.get_barrier_semaphore()
    for offset in range(1, 8):
        for target in (member_device(offset), row_device(offset)):
            pl.semaphore_signal(barrier, inc=1, device_id=target, device_id_type=MESH)
    pl.semaphore_wait(barrier, 14)

    own = [q_ref, d_ref, nd_ref, rf_ref]

    def zslot(part, slot):
        if part < 2:
            return qd_out.at[slot, part]
        return (nd_out, rf_out)[part - 2].at[slot]

    def zcopy(way, step, part):
        slot = lax.rem(z + (NZ - step + 1 if way == 0 else step - 1), NZ)
        return pltpu.make_async_remote_copy(
            src_ref=own[part] if step == 1 else zslot(part, slot),
            dst_ref=zslot(part, slot),
            send_sem=zsend.at[way, step - 1, part],
            recv_sem=zrecv.at[way, step - 1, part],
            device_id=zdev[way],
            device_id_type=MESH,
        )

    def zparts(way, step):
        if step < 4:
            return (0, 2, 3, 1)
        return (0, 2, 3) if way == 0 else (1,)

    def ycopy(way, step, part):
        row = lax.rem(y + ((NY if step == 1 else NY - 1) if way == 0 else step - 1), NY)
        slot = row * NC + c
        return pltpu.make_async_remote_copy(
            src_ref=(k_ref, v_ref)[part] if step == 1 else kv_out.at[slot, part],
            dst_ref=kv_out.at[slot, part],
            send_sem=ysend.at[way, step - 1, part],
            recv_sem=yrecv.at[way, step - 1, part],
            device_id=ydev[way],
            device_id_type=MESH,
        )

    def ccopy(offset, part):
        slot = lax.rem(y + offset, NY) * NC + c
        return pltpu.make_async_remote_copy(
            src_ref=(k_ref, v_ref)[part] if offset == 0 else kv_out.at[slot, part],
            dst_ref=kv_out.at[slot, part],
            send_sem=csend.at[offset, part],
            recv_sem=crecv.at[offset, part],
            device_id=cdev,
            device_id_type=MESH,
        )

    def small(phase, offset):
        over_column = phase in (0, 3, 4)
        other = member(offset) if over_column else lax.rem(z + offset, NZ)
        source, target = (
            (cand_ref.at[other], g1in.at[offset]),
            (s1.at[other], g2in.at[offset]),
            (s2, g3in.at[offset]),
            (gkv.at[me], gkv.at[me]),
            (gacc.at[other], r1in.at[offset]),
            (t1.at[other], r2in.at[offset]),
            (t2, r3in.at[offset]),
        )[phase]
        return pltpu.make_async_remote_copy(
            src_ref=source,
            dst_ref=target,
            send_sem=gsend.at[phase, offset],
            recv_sem=grecv.at[phase, offset],
            device_id=member_device(offset) if over_column else row_device(offset),
            device_id_type=MESH,
        )

    def small_start(phase):
        for offset in range(1, 8):
            small(phase, offset).start()

    def small_wait(phase):
        for offset in range(1, 8):
            small(phase, offset).wait_recv()

    def zstart(step, parts):
        for part in parts:
            for way in (0, 1):
                if part in zparts(way, step):
                    zcopy(way, step, part).start()

    def zpass(step, parts):
        for part in parts:
            for way in (0, 1):
                if part in zparts(way, step):
                    zcopy(way, step, part).wait_recv()
                    if step < 4 and part in zparts(way, step + 1):
                        zcopy(way, step + 1, part).start()

    def block_rows(b):
        return pl.ds(pl.multiple_of(b * BLOCK, BLOCK), BLOCK)

    def window(first, end):
        @pl.loop(first, end)
        def _(i):
            up = (i >= blocks).astype(jnp.int32)
            down = (i >= 2 * blocks - 1).astype(jnp.int32)
            low = i - up * blocks - down * (blocks - 1)
            qb = low + down
            kb = low + up - down
            rows, krows = block_rows(qb), block_rows(kb)
            dq, dk, dv = pair_terms(
                q_ref[rows, :], d_ref[rows, :], query_rows(nd_ref[qb // 2], qb), k_ref[krows, :], v_ref[krows, :], factor
            )
            dq_out[rows, :] += dq
            dk_out[krows, :] += dk
            dv_out[krows, :] += dv

    def whole(g):
        gk = jnp.concatenate([gkv[4 * g], gkv[4 * g + 1]], axis=0)
        gv = jnp.concatenate([gkv[4 * g + 2], gkv[4 * g + 3]], axis=0)

        @pl.loop(0, blocks)
        def _(b):
            rows = block_rows(b)
            dq, dk, dv = pair_terms(
                q_ref[rows, :], d_ref[rows, :], query_rows(nd_ref[b // 2], b), gk, gv, factor
            )
            dq_out[rows, :] += dq
            gacc[4 * g] += dk[:half]
            gacc[4 * g + 1] += dk[half:]
            gacc[4 * g + 2] += dv[:half]
            gacc[4 * g + 3] += dv[half:]

    zstart(1, (0,))
    small_start(0)
    local = [
        pltpu.make_async_copy(q_ref, qd_out.at[z, 0], lsem.at[0]),
        pltpu.make_async_copy(d_ref, qd_out.at[z, 1], lsem.at[1]),
        pltpu.make_async_copy(nd_ref, nd_out.at[z], lsem.at[2]),
        pltpu.make_async_copy(rf_ref, rf_out.at[z], lsem.at[3]),
        pltpu.make_async_copy(k_ref, kv_out.at[me, 0], lsem.at[4]),
        pltpu.make_async_copy(v_ref, kv_out.at[me, 1], lsem.at[5]),
    ]
    for copy in local:
        copy.start()

    @pl.loop(0, blocks)
    def _(b):
        zero = jnp.zeros((BLOCK, q_ref.shape[1]), F32)
        dq_out[block_rows(b), :] = zero
        dk_out[block_rows(b), :] = zero
        dv_out[block_rows(b), :] = zero
        gacc[b] = zero[:half]

    window(0, 2)
    small_wait(0)
    slice_sum = cand_ref[me].astype(F32)
    for offset in range(1, 8):
        slice_sum = slice_sum + g1in[offset].astype(F32)
    s1[...] = slice_sum.astype(BF16).reshape(s1.shape)
    zstart(1, (2, 3, 1))
    window(2, 4)
    small_start(1)
    window(4, 7)
    small_wait(1)
    part_sum = s1[z].astype(F32)
    for offset in range(1, 8):
        part_sum = part_sum + g2in[offset].astype(F32)
    s2[...] = part_sum.astype(BF16)
    window(7, 8)
    small_start(2)
    zpass(1, (0,))
    window(8, 11)
    small_wait(2)
    s3[z] = s2[...]
    for offset in range(1, 8):
        s3[lax.rem(z + NZ - offset, NZ)] = g3in[offset]
    gkv[me] = s3[...].reshape(gkv.shape[1:])
    window(11, 13)
    small_start(3)
    for part in (0, 1):
        for way in (0, 1):
            ycopy(way, 1, part).start()
        ccopy(0, part).start()
    zpass(1, (2, 3, 1))
    window(13, 16)
    small_wait(3)
    whole(0)
    zpass(2, (0,))
    whole(1)
    for part in (0, 1):
        for way in (0, 1):
            ycopy(way, 1, part).wait_recv()
            if part == way:
                ycopy(way, 2, part).start()
            ccopy(NY - 1 if way == 0 else 1, part).start()
    small_start(4)
    zpass(2, (2, 3, 1))
    window(16, 19)
    small_wait(4)
    slice_sum = gacc[me]
    for offset in range(1, 8):
        slice_sum = slice_sum + r1in[offset]
    t1[...] = slice_sum.reshape(t1.shape)
    window(19, 21)
    small_start(5)
    for way in (0, 1):
        ycopy(way, 2, way).wait_recv()
        ccopy(2, way).start()
    zpass(3, (0,))
    window(21, 22)
    small_wait(5)
    part_sum = t1[z]
    for offset in range(1, 8):
        part_sum = part_sum + r2in[offset]
    t2[...] = part_sum
    zpass(3, (2, 3, 1))
    small_start(6)
    small_wait(6)
    total_out[z] = t2[...]
    for offset in range(1, 8):
        total_out[lax.rem(z + NZ - offset, NZ)] = r3in[offset]
    zpass(4, (0, 2, 3, 1))
    for offset in range(NY):
        for part in (0, 1):
            ccopy(offset, part).wait()
    for way in (0, 1):
        for step in range(1, 5):
            for part in zparts(way, step):
                zcopy(way, step, part).wait_send()
        for part in (0, 1):
            ycopy(way, 1, part).wait_send()
        ycopy(way, 2, way).wait_send()
    for phase in range(7):
        for offset in range(1, 8):
            small(phase, offset).wait_send()
    for copy in local:
        copy.wait()


def pair_kernel(
    glob_ref, rf_hbm, qd_hbm, kv_hbm, nd_hbm, total_ref, dq_out, dkv_out,
    dq_acc, dk_acc, dv_acc, qd_ref, kv_ref, nd_ref, rf_ref, list_ref, sem,
    *, factor,
):
    y, z, c = place()
    blocks = qd_ref.shape[2] // BLOCK
    grid = NZ * blocks
    copies = [
        pltpu.make_async_copy(rf_hbm, rf_ref, sem.at[0]),
        pltpu.make_async_copy(nd_hbm, nd_ref, sem.at[1]),
        pltpu.make_async_copy(qd_hbm, qd_ref, sem.at[2]),
        pltpu.make_async_copy(kv_hbm, kv_ref, sem.at[3]),
    ]
    for copy in copies:
        copy.start()

    @pl.loop(0, grid)
    def _(i):
        zero = jnp.zeros((BLOCK, qd_ref.shape[3]), F32)
        dq_acc[i] = zero
        dk_acc[i] = zero
        dv_acc[i] = zero

    half = BLOCK // 2
    for g in range(2):
        owner = glob_ref[g] // blocks
        column = lax.rem(owner // NC, NZ)
        member = (owner // (NC * NZ)) * NC + lax.rem(owner, NC)
        slot = member * blocks + lax.rem(glob_ref[g], blocks)
        mine = jnp.logical_and(column == z, (y * NC + c) // 4 == g)
        total = total_ref[...].reshape(half, total_ref.shape[2])
        rows = pl.ds(pl.multiple_of(c * half, half), half)

        @pl.when(jnp.logical_and(mine, lax.rem(y, 2) == 0))
        def _():
            dk_acc[slot, rows, :] += total

        @pl.when(jnp.logical_and(mine, lax.rem(y, 2) == 1))
        def _():
            dv_acc[slot, rows, :] += total

    def window_item(n, slot, b, seq, key_block, wanted):
        member = (seq // (NC * NZ)) * NC + lax.rem(seq, NC)
        list_ref[n] = ((slot * blocks + b) << 8) | ((member * blocks + key_block) << 1)
        return n + wanted.astype(jnp.int32)

    seq = (y * NZ + z) * NC + c
    nearby = jnp.where(c == 0, seq + 1, seq - 1)
    count = window_item(
        jnp.int32(0), z, jnp.where(c == 0, blocks - 1, 0), nearby, jnp.where(c == 0, 0, blocks - 1), seq >= 0
    )
    far_slot = jnp.where(c == 0, lax.rem(z + 1, NZ), lax.rem(z + NZ - 1, NZ))
    far_seq = (y * NZ + far_slot) * NC + c
    far_key = jnp.where(c == 0, far_seq - 1, far_seq + 1)
    inside = jnp.logical_and(far_key >= 0, far_key < NY * NZ * NC)
    count = window_item(
        count, far_slot, jnp.where(c == 0, 0, blocks - 1),
        jnp.clip(far_key, 0, NY * NZ * NC - 1), jnp.where(c == 0, blocks - 1, 0), inside,
    )

    copies[0].wait()

    def per_slot(slot, n):
        for b in range(blocks):
            for r in range(3):
                code = rf_ref[slot, r, b]
                list_ref[n] = ((slot * blocks + b) << 8) | ((code & (grid - 1)) << 1)
                n = n + ((code >> 6) == z).astype(jnp.int32)
        return n

    count = lax.fori_loop(0, NZ, per_slot, count)
    list_ref[count] = jnp.int32(1)
    for copy in copies[1:]:
        copy.wait()

    def terms(item):
        query, key = item >> 8, (item >> 1) & (grid - 1)
        qs, qb = query >> 3, query & (blocks - 1)
        ks, kb = key >> 3, key & (blocks - 1)
        qrows = pl.ds(pl.multiple_of(qb * BLOCK, BLOCK), BLOCK)
        krows = pl.ds(pl.multiple_of(kb * BLOCK, BLOCK), BLOCK)
        return pair_terms(
            qd_ref[qs, 0, qrows, :],
            qd_ref[qs, 1, qrows, :],
            query_rows(nd_ref[qs, qb >> 1], qb),
            kv_ref[ks, 0, krows, :],
            kv_ref[ks, 1, krows, :],
            factor,
        )

    @pl.loop(0, (count + 1) // 2)
    def _(i):
        items = [list_ref[2 * i], list_ref[2 * i + 1]]
        sums = [terms(item) for item in items]
        for item, (dq, dk, dv) in zip(items, sums):
            spare = (item & 1) * grid
            dq_acc[(item >> 8) + spare] += dq
            dk_acc[((item >> 1) & (grid - 1)) + spare] += dk
            dv_acc[((item >> 1) & (grid - 1)) + spare] += dv

    @pl.loop(0, grid)
    def _(i):
        slot = i >> 3
        rows = pl.ds(pl.multiple_of((i & (blocks - 1)) * BLOCK, BLOCK), BLOCK)
        dq_out[slot, rows, :] = dq_acc[i].astype(BF16)
        dkv_out[slot, 0, rows, :] = (dk_acc[i] * factor).astype(BF16)
        dkv_out[slot, 1, rows, :] = dv_acc[i].astype(BF16)


def reduce_kernel(
    dq_in, dkv_in, dq_own, dk_own, dv_own, dq_out, dk_out, dv_out,
    zbuf, zin, cin, csum, ybuf, yin,
    zsend, zrecv, ysend, yrecv, csend, crecv,
    *, factor,
):
    y, z, c = place()
    half = dq_out.shape[0] // 2
    zdev = [device(y, lax.rem(z + 1, NZ), c), device(y, lax.rem(z + NZ - 1, NZ), c)]
    ydev = [device(lax.rem(y + 1, NY), z, c), device(lax.rem(y + NY - 1, NY), z, c)]
    cdev = device(y, z, 1 - c)

    barrier = pltpu.get_barrier_semaphore()
    for target in zdev + ydev + [cdev]:
        pl.semaphore_signal(barrier, inc=1, device_id=target, device_id_type=MESH)
    pl.semaphore_wait(barrier, 5)

    def zparts(way, step):
        return (way,) if step == 1 else (0, 1)

    def zplain(way, step, part):
        return step == 1 or (step == 2 and part != way)

    def ztarget(way, step):
        return lax.rem(z + (5 - step if way == 0 else NZ - 5 + step), NZ)

    def zcopy(way, step, part):
        rows = pl.ds(part * half, half)
        if zplain(way, step, part):
            source = dq_in.at[ztarget(way, step), rows]
        else:
            source = zbuf.at[way, step - 1, rows]
        return pltpu.make_async_remote_copy(
            src_ref=source,
            dst_ref=zin.at[way, step - 1, rows],
            send_sem=zsend.at[way, step - 1, part],
            recv_sem=zrecv.at[way, step - 1, part],
            device_id=zdev[way],
            device_id_type=MESH,
        )

    def ccopy(offset, part):
        row = lax.rem(y + offset, NY)
        return pltpu.make_async_remote_copy(
            src_ref=dkv_in.at[row * NC + 1 - c, part],
            dst_ref=cin.at[offset, part],
            send_sem=csend.at[offset, part],
            recv_sem=crecv.at[offset, part],
            device_id=cdev,
            device_id_type=MESH,
        )

    def ycopy(way, step, part):
        return pltpu.make_async_remote_copy(
            src_ref=csum.at[2, part] if step == 1 else ybuf.at[way, part],
            dst_ref=yin.at[way, step - 1, part],
            send_sem=ysend.at[way, step - 1, part],
            recv_sem=yrecv.at[way, step - 1, part],
            device_id=ydev[way],
            device_id_type=MESH,
        )

    for offset in (2, 1, 3, 0):
        for part in (0, 1):
            ccopy(offset, part).start()
    for way in (0, 1):
        zcopy(way, 1, way).start()
        zcopy(way, 2, 1 - way).start()

    def zround(step):
        for part in (0, 1):
            for way in (0, 1):
                if part in zparts(way, step):
                    zcopy(way, step, part).wait_recv()
                    rows = pl.ds(part * half, half)
                    mine = dq_in[ztarget(way, step + 1), rows, :].astype(F32)
                    zbuf[way, step, rows, :] = (mine + zin[way, step - 1, rows, :].astype(F32)).astype(BF16)
                    zcopy(way, step + 1, part).start()

    def cadd(offset, part):
        ccopy(offset, part).wait_recv()
        row = lax.rem(y + offset, NY)
        mine = dkv_in[row * NC + c, part].astype(F32)
        return mine + cin[offset, part].astype(F32)

    for part in (0, 1):
        csum[2, part] = cadd(2, part).astype(BF16)
        ycopy(part, 1, part).start()
    zround(1)
    for way in (0, 1):
        offset = 1 if way == 0 else NY - 1
        for part in (1 - way, way):
            total = cadd(offset, part)
            if part == way:
                ycopy(way, 1, part).wait_recv()
                total = total + yin[way, 0, part].astype(F32)
            ybuf[way, part] = total.astype(BF16)
            ycopy(way, 2, part).start()
    zround(2)
    zround(3)
    for part, out in ((0, dk_out), (1, dv_out)):
        total = cadd(0, part) + (dk_own[...] * factor if part == 0 else dv_own[...])
        for way in (0, 1):
            ycopy(way, 2, part).wait_recv()
            total = total + yin[way, 1, part].astype(F32)
        out[...] = total.astype(BF16)
    for part in (0, 1):
        rows = pl.ds(part * half, half)
        total = dq_in[z, rows, :].astype(F32) + dq_own[rows, :]
        for way in (0, 1):
            zcopy(way, 4, part).wait_recv()
            total = total + zin[way, 3, rows, :].astype(F32)
        dq_out[rows, :] = total.astype(BF16)
    for way in (0, 1):
        for step in range(1, 5):
            for part in zparts(way, step):
                zcopy(way, step, part).wait_send()
        ycopy(way, 1, way).wait_send()
        for part in (0, 1):
            ycopy(way, 2, part).wait_send()
    for offset in range(NY):
        for part in (0, 1):
            ccopy(offset, part).wait_send()


def shards(queries, keys, values, outputs, d_outputs, log_norm, rand_owner, rand_local, glob_blocks):
    tokens, features = queries.shape
    blocks = tokens // BLOCK
    factor = 1.0 / math.sqrt(features // log_norm.shape[0])
    vmem = pl.BlockSpec(memory_space=pltpu.VMEM)
    smem = pl.BlockSpec(memory_space=pltpu.SMEM)
    anywhere = pl.BlockSpec(memory_space=pl.ANY)
    dma = pltpu.SemaphoreType.DMA

    side, refs, cand = pl.pallas_call(
        side_kernel,
        out_shape=(
            jax.ShapeDtypeStruct((blocks // 2, 8, BLOCK), F32),
            jax.ShapeDtypeStruct((8, BLOCK), jnp.int32),
            jax.ShapeDtypeStruct((8, BLOCK // 2, features), BF16),
        ),
        in_specs=[vmem] * 7 + [smem],
        out_specs=(vmem,) * 3,
        name="side",
    )(outputs, d_outputs, log_norm, rand_owner.T, rand_local.T, keys, values, glob_blocks)

    slices = (8, BLOCK // 2, features)
    eighths = (8, BLOCK // 16, features)
    qd, kv, nd, rf, dq_own, dk_own, dv_own, total = pl.pallas_call(
        functools.partial(gather_kernel, factor=factor),
        out_shape=(
            jax.ShapeDtypeStruct((NZ, 2, tokens, features), BF16),
            jax.ShapeDtypeStruct((NY * NC, 2, tokens, features), BF16),
            jax.ShapeDtypeStruct((NZ, blocks // 2, 8, BLOCK), F32),
            jax.ShapeDtypeStruct((NZ, 8, BLOCK), jnp.int32),
            jax.ShapeDtypeStruct((tokens, features), F32),
            jax.ShapeDtypeStruct((tokens, features), F32),
            jax.ShapeDtypeStruct((tokens, features), F32),
            jax.ShapeDtypeStruct(eighths, F32),
        ),
        in_specs=[vmem] * 7,
        out_specs=(anywhere,) * 4 + (vmem,) * 4,
        scratch_shapes=[
            pltpu.VMEM(slices, BF16), pltpu.VMEM(eighths, BF16), pltpu.VMEM(eighths, BF16),
            pltpu.VMEM(eighths[1:], BF16), pltpu.VMEM(eighths, BF16), pltpu.VMEM(eighths, BF16),
            pltpu.VMEM(slices, BF16), pltpu.VMEM(slices, F32), pltpu.VMEM(slices, F32),
            pltpu.VMEM(eighths, F32), pltpu.VMEM(eighths, F32), pltpu.VMEM(eighths[1:], F32),
            pltpu.VMEM(eighths, F32),
            dma((2, 4, 4)), dma((2, 4, 4)), dma((2, 2, 2)), dma((2, 2, 2)),
            dma((NY, 2)), dma((NY, 2)), dma((7, 8)), dma((7, 8)), dma((6,)),
        ],
        compiler_params=pltpu.CompilerParams(collective_id=0, has_side_effects=True, vmem_limit_bytes=12 * MIB),
        name="gather",
    )(queries, d_outputs, keys, values, side, refs, cand)

    dq_part, dkv_part = pl.pallas_call(
        functools.partial(pair_kernel, factor=factor),
        out_shape=(
            jax.ShapeDtypeStruct((NZ, tokens, features), BF16),
            jax.ShapeDtypeStruct((NY * NC, 2, tokens, features), BF16),
        ),
        in_specs=[smem, anywhere, anywhere, anywhere, anywhere, vmem],
        out_specs=(vmem, vmem),
        scratch_shapes=[
            pltpu.VMEM((NZ * blocks + 1, BLOCK, features), F32),
            pltpu.VMEM((NY * NC * blocks + 1, BLOCK, features), F32),
            pltpu.VMEM((NY * NC * blocks + 1, BLOCK, features), F32),
            pltpu.VMEM((NZ, 2, tokens, features), BF16),
            pltpu.VMEM((NY * NC, 2, tokens, features), BF16),
            pltpu.VMEM((NZ, blocks // 2, 8, BLOCK), F32),
            pltpu.SMEM((NZ, 8, BLOCK), jnp.int32),
            pltpu.SMEM((256,), jnp.int32),
            dma((4,)),
        ],
        compiler_params=pltpu.CompilerParams(vmem_limit_bytes=32 * MIB),
        name="pairs",
    )(glob_blocks, rf, qd, kv, nd, total)

    return tuple(pl.pallas_call(
        functools.partial(reduce_kernel, factor=factor),
        out_shape=(jax.ShapeDtypeStruct((tokens, features), BF16),) * 3,
        in_specs=[vmem] * 5,
        out_specs=(vmem,) * 3,
        scratch_shapes=[
            pltpu.VMEM((2, 4, tokens, features), BF16),
            pltpu.VMEM((2, 4, tokens, features), BF16),
            pltpu.VMEM((NY, 2, tokens, features), BF16),
            pltpu.VMEM((NY, 2, tokens, features), BF16),
            pltpu.VMEM((2, 2, tokens, features), BF16),
            pltpu.VMEM((2, 2, 2, tokens, features), BF16),
            dma((2, 4, 2)), dma((2, 4, 2)), dma((2, 2, 2)), dma((2, 2, 2)), dma((NY, 2)), dma((NY, 2)),
        ],
        compiler_params=pltpu.CompilerParams(collective_id=1, has_side_effects=True, vmem_limit_bytes=24 * MIB),
        name="reduce",
    )(dq_part, dkv_part, dq_own, dk_own, dv_own))


def solution(mesh):
    placed = (
        P("seq", "head"), P("seq", "head"), P("seq", "head"), P("seq", "head"), P("seq", "head"),
        P("head", "seq"), P("seq", None), P("seq", None), P(),
    )
    return jax.shard_map(
        shards,
        mesh=mesh,
        in_specs=placed,
        out_specs=(P("seq", "head"), P("seq", "head"), P("seq", "head")),
        check_vma=False,
    )
```

time: 152 us -> 123 us (0.81)
  Pallas kernels: 144 us -> 113 us
  local copies, waits for them, and re-layouts: 7.16 us -> 8.86 us
    pallas_call x1, Pallas kernels: 40.4 us -> 10.9 us  [shards(): pl.pallas_call(functools.partial(pair_kernel, factor=factor), out_shape=(...]
    unnamed x11 -> x19, local copies, waits for them, and re-layouts: 7.16 us -> 8.86 us
where the time goes in v2:
time: 123 us
  Pallas kernels  113 us (92%)
  local copies, waits for them, and re-layouts  8.86 us (7%)
    pallas_call x1, Pallas kernels, shards(): pl.pallas_call(functools.partial(gather_kernel, factor=factor), out_shape...  66.2 us
    pallas_call x1, Pallas kernels, shards(): pl.pallas_call(functools.partial(reduce_kernel, factor=factor), out_shape...  33.9 us
    pallas_call x1, Pallas kernels, shards(): pl.pallas_call(functools.partial(pair_kernel, factor=factor), out_shape=(...  10.9 us
    unnamed x19, local copies, waits for them, and re-layouts  8.86 us

profile of v2, /device:TPU:1, one launch (start us, length us, event | category | flops | bytes accessed | tf_op | source)
XLA Modules:
  0.0 122.6 jit_solution(2252386900173675710)
XLA Ops:
  0.6 2.1 %side.1 = (f32[4,8,128]{2,1,0:T(8,128)}, s32[8,128]{1,0:T(8,128)}, bf16[8,64,128]{2,1,0:T(8,128)(2,1)}) custom-call(bf16[1024,128]{1,0:T(8,128)(2,1)} %out_ref.1, bf16[1024,128]{1,0:T(8,128)(2,1)} %d_ref.1, f32[2,1024]{1,0:T(2,128)} %norm_ref.1, s32[3,8]{1,0:T(4,128)} %bitcast.2, s32[3,8]{1,0:T(4,128)} %bitcast.3, bf16[1024,128]{1,0:T(8,128)(2,1)} %k_ref.1, ...), custom_call_target="tpu_custom_call" | custom-call | tf_op jit(solution)/shard_map/side/pallas_call | solution.py:601
  2.7 0.0 copy-start
  2.7 0.9 copy-done
  3.7 0.0 copy-start.1
  3.7 0.9 copy-done.1
  4.6 0.0 copy-start.2
  4.6 0.9 copy-done.2
  5.6 0.0 copy-start.3
  5.6 0.9 copy-done.3
  6.5 0.0 copy-start.4
  6.5 0.9 copy-done.4
  7.4 0.0 copy-start.5
  7.4 0.7 copy-done.5
  8.1 0.0 copy-start.6
  8.1 0.7 copy-done.6
  8.8 66.2 %gather.1 = (bf16[8,2,1024,128]{3,2,1,0:T(8,128)(2,1)S(1)}, bf16[8,2,1024,128]{3,2,1,0:T(8,128)(2,1)S(1)}, f32[8,4,8,128]{3,2,1,0:T(8,128)S(1)}, s32[8,8,128]{2,...) custom-call(bf16[1024,128]{1,0:T(8,128)(2,1)S(1)} %copy-done.3, ...), custom_call_target="tpu_custom_call" | custom-call | tf_op jit(solution)/shard_map/gather/pallas_call | solution.py:615
  75.0 0.0 copy-start.7
  75.0 0.6 copy-done.7
  75.7 10.9 %pairs.1 = (bf16[8,1024,128]{2,1,0:T(8,128)(2,1)S(1)}, bf16[8,2,1024,128]{3,2,1,0:T(8,128)(2,1)S(1)}) custom-call(s32[2]{0:T(128)S(1)} %copy-done.7, s32[8,8,128]{2,1,0:T(8,128)S(1)} %get-tuple-element.19.rf_hbm, bf16[8,2,1024,128]{3,2,1,0:T(8,128)(2,1)S(1)} %get-tuple-element.20.qd_hbm, bf16[8,2,1024,128]{3,2,1,0:T(8,128)(2,1)S(1)} %get-tuple-element.21.kv_hbm, ...), custom_call_target="tpu_custom_call" | custom-call | tf_op jit(solution)/shard_map/pairs/pallas_call | solution.py:642
  86.6 33.9 %reduce.1 = (bf16[1024,128]{1,0:T(8,128)(2,1)S(1)}, bf16[1024,128]{1,0:T(8,128)(2,1)S(1)}, bf16[1024,128]{1,0:T(8,128)(2,1)S(1)}) custom-call(bf16[8,1024,128]{2,1,0:T(8,128)(2,1)S(1)} %get-tuple-element.24.dq_in, bf16[8,2,1024,128]{3,2,1,0:T(8,128)(2,1)S(1)} %get-tuple-element.25.dkv_in, f32[1024,128]{1,0:T(8,128)S(1)} %get-tuple-element.26.dq_own, ...), custom_call_target="tpu_custom_call" | custom-call | tf_op jit(solution)/shard_map/reduce/pallas_call | solution.py:665
  120.5 0.7 copy.15
  121.2 0.7 copy.16
  121.9 0.7 copy.17
Async XLA Ops:
  2.7 0.9 copy-start
  3.7 0.9 copy-start.1
  4.6 0.9 copy-start.2
  5.6 0.9 copy-start.3
  6.5 0.9 copy-start.4
  7.4 0.7 copy-start.5
  8.1 0.7 copy-start.6
  75.0 0.7 copy-start.7

commit v3 on v2

--- a/solution.py
+++ b/solution.py
@@ -28,63 +28,29 @@
     return {"seq": (y * NZ + z) * NC + core}
 
 
-def side_kernel(
-    out_ref, grad_ref, norm_ref, owner_ref, local_ref, key_ref, value_ref, glob_ref, nd_ref, refs_ref, cand_ref
-):
-    blocks = out_ref.shape[0] // BLOCK
-    for b in range(blocks):
-        rows = pl.ds(b * BLOCK, BLOCK)
-        product = out_ref[rows, :].astype(F32) * grad_ref[rows, :].astype(F32)
-        turned = product.T
-        half = turned.shape[0] // 2
-        first = 4 * (b % 2)
-        nd_ref[b // 2, first : first + 2, :] = norm_ref[:, rows]
-        nd_ref[b // 2, first + 2 : first + 3, :] = jnp.sum(turned[:half], axis=0, keepdims=True)
-        nd_ref[b // 2, first + 3 : first + 4, :] = jnp.sum(turned[half:], axis=0, keepdims=True)
-    owner = owner_ref[...]
-    column = jnp.bitwise_and(owner >> 1, NZ - 1)
-    member = (owner >> 4) * NC + jnp.bitwise_and(owner, 1)
-    refs_ref[...] = jnp.zeros(refs_ref.shape, jnp.int32)
-    refs_ref[0:3, 0:blocks] = (column * (NY * NC) + member) * blocks + local_ref[...]
-    seq = lax.axis_index("seq")
-    half = BLOCK // 2
-    for g in range(2):
-        where = glob_ref[g]
-        mine = (where // blocks) == seq
-        start = pl.multiple_of(lax.rem(where, blocks) * BLOCK, BLOCK)
-        for i, ref in enumerate((key_ref, value_ref)):
-            block = ref[pl.ds(start, BLOCK), :]
-            block = jnp.where(mine, block, jnp.zeros_like(block))
-            cand_ref[4 * g + 2 * i] = block[:half]
-            cand_ref[4 * g + 2 * i + 1] = block[half:]
-
-
-def pair_terms(q, d, nd, k, v, factor):
-    lane = lax.broadcasted_iota(jnp.int32, k.shape, 1)
-    half = k.shape[1] // 2
+def per_head(x):
+    lane = lax.broadcasted_iota(jnp.int32, x.shape, 1)
+    zero = jnp.zeros_like(x)
+    low = lane < x.shape[1] // 2
+    return jnp.concatenate([jnp.where(low, x, zero), jnp.where(low, zero, x)], axis=0)
+
+
+def pair_terms(q2, d2, nd, k, v, factor):
+    k = k * factor
     rows = k.shape[0]
-    zero = jnp.zeros_like(k)
-    k = k * factor
-    k2 = jnp.concatenate([jnp.where(lane < half, k, zero), jnp.where(lane < half, zero, k)], axis=0)
-    v2 = jnp.concatenate([jnp.where(lane < half, v, zero), jnp.where(lane < half, zero, v)], axis=0)
     across = (((1,), (1,)), ((), ()))
-    scores = lax.dot_general(k2, q, across, preferred_element_type=F32)
-    grads = lax.dot_general(v2, d, across, preferred_element_type=F32)
-
-    def per_head(first):
-        return jnp.concatenate(
-            [jnp.broadcast_to(nd[i : i + 1, :], (rows, BLOCK)) for i in (first, first + 1)], axis=0
-        )
-
-    weights = jnp.exp(scores - per_head(0))
-    grad_scores = weights * (grads - per_head(2))
+    scores = lax.dot_general(k, q2, across, preferred_element_type=F32)
+    grads = lax.dot_general(v, d2, across, preferred_element_type=F32)
+    norm = jnp.concatenate([nd[0:1], nd[1:2]], axis=1)
+    delta = jnp.concatenate([nd[2:3], nd[3:4]], axis=1)
+    weights = jnp.exp(scores - norm)
+    grad_scores = weights * (grads - delta)
     weights_low = weights.astype(BF16)
     scores_low = grad_scores.astype(BF16)
-    dv2 = jnp.dot(weights_low, d, preferred_element_type=F32)
-    dk2 = jnp.dot(scores_low, q, preferred_element_type=F32)
-    dq = lax.dot_general(scores_low, k2, (((0,), (0,)), ((), ())), preferred_element_type=F32)
-    dv = jnp.where(lane < half, dv2[:rows], dv2[rows:])
-    dk = jnp.where(lane < half, dk2[:rows], dk2[rows:])
+    dv = jnp.dot(weights_low, d2, preferred_element_type=F32)
+    dk = jnp.dot(scores_low, q2, preferred_element_type=F32)
+    both = jnp.concatenate([scores_low[:, :BLOCK], scores_low[:, BLOCK:]], axis=0)
+    dq = lax.dot_general(both, per_head(k), (((0,), (0,)), ((), ())), preferred_element_type=F32)
     return dq, dk, dv
 
 
@@ -93,15 +59,25 @@
 
 
 def gather_kernel(
-    q_ref, d_ref, k_ref, v_ref, nd_ref, rf_ref, cand_ref,
+    q_hbm, d_hbm, k_hbm, v_hbm, o_hbm, norm_ref, owner_ref, local_ref, glob_ref,
     qd_out, kv_out, nd_out, rf_out, dq_out, dk_out, dv_out, total_out,
+    q_ref, d_ref, k_ref, v_ref, o_ref, nd_ref, rf_ref, cand_ref,
     g1in, s1, g2in, s2, g3in, s3, gkv, gacc, r1in, t1, r2in, t2, r3in,
     zsend, zrecv, ysend, yrecv, csend, crecv, gsend, grecv, lsem,
     *, factor,
 ):
     y, z, c = place()
-    blocks = q_ref.shape[0] // BLOCK
+    tokens = q_ref.shape[0]
+    blocks = tokens // BLOCK
     half = BLOCK // 2
+    loads = [
+        pltpu.make_async_copy(source, target, lsem.at[i])
+        for i, (source, target) in enumerate(
+            ((k_hbm, k_ref), (v_hbm, v_ref), (o_hbm, o_ref), (d_hbm, d_ref), (q_hbm, q_ref))
+        )
+    ]
+    for copy in loads:
+        copy.start()
     zdev = [device(y, lax.rem(z + 1, NZ), c), device(y, lax.rem(z + NZ - 1, NZ), c)]
     ydev = [device(lax.rem(y + 1, NY), z, c), device(lax.rem(y + NY - 1, NY), z, c)]
     cdev = device(y, z, 1 - c)
@@ -123,18 +99,21 @@
             pl.semaphore_signal(barrier, inc=1, device_id=target, device_id_type=MESH)
     pl.semaphore_wait(barrier, 14)
 
-    own = [q_ref, d_ref, nd_ref, rf_ref]
-
-    def zslot(part, slot):
-        if part < 2:
-            return qd_out.at[slot, part]
-        return (nd_out, rf_out)[part - 2].at[slot]
+    def zwhere(part, slot):
+        if part < 4:
+            return qd_out.at[slot, part // 2, pl.ds((part % 2) * tokens // 2, tokens // 2)]
+        return (nd_out, rf_out)[part - 4].at[slot]
+
+    def zown(part):
+        if part < 4:
+            return (q_hbm, d_hbm)[part // 2].at[pl.ds((part % 2) * tokens // 2, tokens // 2)]
+        return (nd_ref, rf_ref)[part - 4]
 
     def zcopy(way, step, part):
         slot = lax.rem(z + (NZ - step + 1 if way == 0 else step - 1), NZ)
         return pltpu.make_async_remote_copy(
-            src_ref=own[part] if step == 1 else zslot(part, slot),
-            dst_ref=zslot(part, slot),
+            src_ref=zown(part) if step == 1 else zwhere(part, slot),
+            dst_ref=zwhere(part, slot),
             send_sem=zsend.at[way, step - 1, part],
             recv_sem=zrecv.at[way, step - 1, part],
             device_id=zdev[way],
@@ -143,14 +122,14 @@
 
     def zparts(way, step):
         if step < 4:
-            return (0, 2, 3, 1)
-        return (0, 2, 3) if way == 0 else (1,)
+            return (0, 1, 2, 3, 4, 5)
+        return (0, 1, 4, 5) if way == 0 else (2, 3)
 
     def ycopy(way, step, part):
         row = lax.rem(y + ((NY if step == 1 else NY - 1) if way == 0 else step - 1), NY)
         slot = row * NC + c
         return pltpu.make_async_remote_copy(
-            src_ref=(k_ref, v_ref)[part] if step == 1 else kv_out.at[slot, part],
+            src_ref=(k_hbm, v_hbm)[part] if step == 1 else kv_out.at[slot, part],
             dst_ref=kv_out.at[slot, part],
             send_sem=ysend.at[way, step - 1, part],
             recv_sem=yrecv.at[way, step - 1, part],
@@ -161,7 +140,7 @@
     def ccopy(offset, part):
         slot = lax.rem(y + offset, NY) * NC + c
         return pltpu.make_async_remote_copy(
-            src_ref=(k_ref, v_ref)[part] if offset == 0 else kv_out.at[slot, part],
+            src_ref=(k_hbm, v_hbm)[part] if offset == 0 else kv_out.at[slot, part],
             dst_ref=kv_out.at[slot, part],
             send_sem=csend.at[offset, part],
             recv_sem=crecv.at[offset, part],
@@ -225,37 +204,83 @@
             kb = low + up - down
             rows, krows = block_rows(qb), block_rows(kb)
             dq, dk, dv = pair_terms(
-                q_ref[rows, :], d_ref[rows, :], query_rows(nd_ref[qb // 2], qb), k_ref[krows, :], v_ref[krows, :], factor
+                per_head(q_ref[rows, :]), per_head(d_ref[rows, :]), query_rows(nd_ref[qb // 2], qb),
+                k_ref[krows, :], v_ref[krows, :], factor,
             )
             dq_out[rows, :] += dq
             dk_out[krows, :] += dk
             dv_out[krows, :] += dv
 
-    def whole(g):
-        gk = jnp.concatenate([gkv[4 * g], gkv[4 * g + 1]], axis=0)
-        gv = jnp.concatenate([gkv[4 * g + 2], gkv[4 * g + 3]], axis=0)
-
-        @pl.loop(0, blocks)
-        def _(b):
+    def whole(first, end):
+        @pl.loop(first, end)
+        def _(i):
+            b, g = i // 2, lax.rem(i, 2)
             rows = block_rows(b)
+            part = 4 * g
             dq, dk, dv = pair_terms(
-                q_ref[rows, :], d_ref[rows, :], query_rows(nd_ref[b // 2], b), gk, gv, factor
+                per_head(q_ref[rows, :]), per_head(d_ref[rows, :]), query_rows(nd_ref[b // 2], b),
+                jnp.concatenate([gkv[part], gkv[part + 1]], axis=0),
+                jnp.concatenate([gkv[part + 2], gkv[part + 3]], axis=0),
+                factor,
             )
             dq_out[rows, :] += dq
-            gacc[4 * g] += dk[:half]
-            gacc[4 * g + 1] += dk[half:]
-            gacc[4 * g + 2] += dv[:half]
-            gacc[4 * g + 3] += dv[half:]
+            gacc[part] += dk[:half]
+            gacc[part + 1] += dk[half:]
+            gacc[part + 2] += dv[:half]
+            gacc[part + 3] += dv[half:]
+
+    def ystep1(part):
+        for way in (0, 1):
+            ycopy(way, 1, part).wait_recv()
+            if part == way:
+                ycopy(way, 2, part).start()
+            ccopy(NY - 1 if way == 0 else 1, part).start()
 
     zstart(1, (0,))
+    loads[0].wait()
+    loads[1].wait()
+    seq = lax.axis_index("seq")
+    for g in range(2):
+        local_block = glob_ref[g] - seq * blocks
+        for i, ref in enumerate((k_ref, v_ref)):
+            block = jnp.zeros((BLOCK, k_ref.shape[1]), BF16)
+            for b in range(blocks):
+                block = jnp.where(local_block == b, ref[pl.ds(b * BLOCK, BLOCK), :], block)
+            cand_ref[4 * g + 2 * i] = block[:half]
+            cand_ref[4 * g + 2 * i + 1] = block[half:]
+    owner = owner_ref[...]
+    column = jnp.bitwise_and(owner >> 1, NZ - 1)
+    other = (owner >> 4) * NC + jnp.bitwise_and(owner, 1)
+    rf_ref[...] = jnp.zeros(rf_ref.shape, jnp.int32)
+    rf_ref[0:3, 0:blocks] = (column * (NY * NC) + other) * blocks + local_ref[...]
+    loads[2].wait()
+    loads[3].wait()
+
+    def row_values(b):
+        rows = pl.ds(b * BLOCK, BLOCK)
+        turned = (o_ref[rows, :].astype(F32) * d_ref[rows, :].astype(F32)).T
+        nd_ref[b // 2, 4 * (b % 2) : 4 * (b % 2) + 4, :] = jnp.concatenate(
+            [
+                norm_ref[:, rows],
+                jnp.sum(turned[: turned.shape[0] // 2], axis=0, keepdims=True),
+                jnp.sum(turned[turned.shape[0] // 2 :], axis=0, keepdims=True),
+            ],
+            axis=0,
+        )
+
+    row_values(0)
     small_start(0)
+    zstart(1, (1,))
+    for b in range(1, blocks):
+        row_values(b)
+    loads[4].wait()
     local = [
-        pltpu.make_async_copy(q_ref, qd_out.at[z, 0], lsem.at[0]),
-        pltpu.make_async_copy(d_ref, qd_out.at[z, 1], lsem.at[1]),
-        pltpu.make_async_copy(nd_ref, nd_out.at[z], lsem.at[2]),
-        pltpu.make_async_copy(rf_ref, rf_out.at[z], lsem.at[3]),
-        pltpu.make_async_copy(k_ref, kv_out.at[me, 0], lsem.at[4]),
-        pltpu.make_async_copy(v_ref, kv_out.at[me, 1], lsem.at[5]),
+        pltpu.make_async_copy(q_ref, qd_out.at[z, 0], lsem.at[5]),
+        pltpu.make_async_copy(d_ref, qd_out.at[z, 1], lsem.at[6]),
+        pltpu.make_async_copy(nd_ref, nd_out.at[z], lsem.at[7]),
+        pltpu.make_async_copy(rf_ref, rf_out.at[z], lsem.at[8]),
+        pltpu.make_async_copy(k_ref, kv_out.at[me, 0], lsem.at[9]),
+        pltpu.make_async_copy(v_ref, kv_out.at[me, 1], lsem.at[10]),
     ]
     for copy in local:
         copy.start()
@@ -268,75 +293,80 @@
         dv_out[block_rows(b), :] = zero
         gacc[b] = zero[:half]
 
-    window(0, 2)
     small_wait(0)
     slice_sum = cand_ref[me].astype(F32)
     for offset in range(1, 8):
         slice_sum = slice_sum + g1in[offset].astype(F32)
     s1[...] = slice_sum.astype(BF16).reshape(s1.shape)
-    zstart(1, (2, 3, 1))
+    window(0, 2)
+    small_start(1)
+    zstart(1, (4, 5, 2, 3))
     window(2, 4)
-    small_start(1)
-    window(4, 7)
+    zpass(1, (0,))
+    window(4, 5)
     small_wait(1)
     part_sum = s1[z].astype(F32)
     for offset in range(1, 8):
         part_sum = part_sum + g2in[offset].astype(F32)
     s2[...] = part_sum.astype(BF16)
-    window(7, 8)
+    window(5, 6)
     small_start(2)
-    zpass(1, (0,))
-    window(8, 11)
+    zpass(1, (1, 4, 5))
+    window(6, 9)
+    zpass(1, (2,))
     small_wait(2)
     s3[z] = s2[...]
     for offset in range(1, 8):
         s3[lax.rem(z + NZ - offset, NZ)] = g3in[offset]
     gkv[me] = s3[...].reshape(gkv.shape[1:])
-    window(11, 13)
+    window(9, 11)
     small_start(3)
     for part in (0, 1):
         for way in (0, 1):
             ycopy(way, 1, part).start()
         ccopy(0, part).start()
-    zpass(1, (2, 3, 1))
-    window(13, 16)
+    zpass(1, (3,))
+    window(11, 14)
+    zpass(2, (0,))
     small_wait(3)
-    whole(0)
-    zpass(2, (0,))
-    whole(1)
-    for part in (0, 1):
-        for way in (0, 1):
-            ycopy(way, 1, part).wait_recv()
-            if part == way:
-                ycopy(way, 2, part).start()
-            ccopy(NY - 1 if way == 0 else 1, part).start()
+    whole(0, 4)
+    zpass(2, (1, 4, 5))
+    whole(4, 8)
+    zpass(2, (2,))
+    whole(8, 12)
+    zpass(2, (3,))
+    whole(12, 16)
+    window(14, 15)
+    ystep1(0)
     small_start(4)
-    zpass(2, (2, 3, 1))
-    window(16, 19)
+    zpass(3, (0,))
+    window(15, 17)
+    ystep1(1)
     small_wait(4)
     slice_sum = gacc[me]
     for offset in range(1, 8):
         slice_sum = slice_sum + r1in[offset]
     t1[...] = slice_sum.reshape(t1.shape)
-    window(19, 21)
+    window(17, 19)
     small_start(5)
-    for way in (0, 1):
-        ycopy(way, 2, way).wait_recv()
-        ccopy(2, way).start()
-    zpass(3, (0,))
-    window(21, 22)
+    zpass(3, (1, 4, 5))
+    window(19, 22)
+    zpass(3, (2,))
     small_wait(5)
     part_sum = t1[z]
     for offset in range(1, 8):
         part_sum = part_sum + r2in[offset]
     t2[...] = part_sum
-    zpass(3, (2, 3, 1))
+    for way in (0, 1):
+        ycopy(way, 2, way).wait_recv()
+        ccopy(2, way).start()
     small_start(6)
+    zpass(3, (3,))
     small_wait(6)
     total_out[z] = t2[...]
     for offset in range(1, 8):
         total_out[lax.rem(z + NZ - offset, NZ)] = r3in[offset]
-    zpass(4, (0, 2, 3, 1))
+    zpass(4, (0, 1, 4, 5, 2, 3))
     for offset in range(NY):
         for part in (0, 1):
             ccopy(offset, part).wait()
@@ -355,18 +385,16 @@
 
 
 def pair_kernel(
-    glob_ref, rf_hbm, qd_hbm, kv_hbm, nd_hbm, total_ref, dq_out, dkv_out,
-    dq_acc, dk_acc, dv_acc, qd_ref, kv_ref, nd_ref, rf_ref, list_ref, sem,
+    glob_hbm, rf_any, qd_ref, kv_ref, nd_ref, total_ref, dq_out, dkv_out,
+    dq_acc, dk_acc, dv_acc, glob_ref, rf_ref, list_ref, sem,
     *, factor,
 ):
     y, z, c = place()
     blocks = qd_ref.shape[2] // BLOCK
     grid = NZ * blocks
     copies = [
-        pltpu.make_async_copy(rf_hbm, rf_ref, sem.at[0]),
-        pltpu.make_async_copy(nd_hbm, nd_ref, sem.at[1]),
-        pltpu.make_async_copy(qd_hbm, qd_ref, sem.at[2]),
-        pltpu.make_async_copy(kv_hbm, kv_ref, sem.at[3]),
+        pltpu.make_async_copy(rf_any, rf_ref, sem.at[0]),
+        pltpu.make_async_copy(glob_hbm, glob_ref, sem.at[1]),
     ]
     for copy in copies:
         copy.start()
@@ -378,6 +406,7 @@
         dk_acc[i] = zero
         dv_acc[i] = zero
 
+    copies[1].wait()
     half = BLOCK // 2
     for g in range(2):
         owner = glob_ref[g] // blocks
@@ -427,8 +456,6 @@
 
     count = lax.fori_loop(0, NZ, per_slot, count)
     list_ref[count] = jnp.int32(1)
-    for copy in copies[1:]:
-        copy.wait()
 
     def terms(item):
         query, key = item >> 8, (item >> 1) & (grid - 1)
@@ -437,8 +464,8 @@
         qrows = pl.ds(pl.multiple_of(qb * BLOCK, BLOCK), BLOCK)
         krows = pl.ds(pl.multiple_of(kb * BLOCK, BLOCK), BLOCK)
         return pair_terms(
-            qd_ref[qs, 0, qrows, :],
-            qd_ref[qs, 1, qrows, :],
+            per_head(qd_ref[qs, 0, qrows, :]),
+            per_head(qd_ref[qs, 1, qrows, :]),
             query_rows(nd_ref[qs, qb >> 1], qb),
             kv_ref[ks, 0, krows, :],
             kv_ref[ks, 1, krows, :],
@@ -593,22 +620,17 @@
     tokens, features = queries.shape
     blocks = tokens // BLOCK
     factor = 1.0 / math.sqrt(features // log_norm.shape[0])
+    queries, keys, values, outputs, d_outputs, log_norm, owner, local, glob_blocks = (
+        pltpu.with_memory_space_constraint(array, pltpu.HBM)
+        for array in (
+            queries, keys, values, outputs, d_outputs, log_norm, rand_owner.T, rand_local.T, glob_blocks
+        )
+    )
     vmem = pl.BlockSpec(memory_space=pltpu.VMEM)
     smem = pl.BlockSpec(memory_space=pltpu.SMEM)
     anywhere = pl.BlockSpec(memory_space=pl.ANY)
+    hbm = pl.BlockSpec(memory_space=pltpu.HBM)
     dma = pltpu.SemaphoreType.DMA
-
-    side, refs, cand = pl.pallas_call(
-        side_kernel,
-        out_shape=(
-            jax.ShapeDtypeStruct((blocks // 2, 8, BLOCK), F32),
-            jax.ShapeDtypeStruct((8, BLOCK), jnp.int32),
-            jax.ShapeDtypeStruct((8, BLOCK // 2, features), BF16),
-        ),
-        in_specs=[vmem] * 7 + [smem],
-        out_specs=(vmem,) * 3,
-        name="side",
-    )(outputs, d_outputs, log_norm, rand_owner.T, rand_local.T, keys, values, glob_blocks)
 
     slices = (8, BLOCK // 2, features)
     eighths = (8, BLOCK // 16, features)
@@ -624,20 +646,24 @@
             jax.ShapeDtypeStruct((tokens, features), F32),
             jax.ShapeDtypeStruct(eighths, F32),
         ),
-        in_specs=[vmem] * 7,
+        in_specs=[hbm] * 5 + [vmem] * 3 + [smem],
         out_specs=(anywhere,) * 4 + (vmem,) * 4,
         scratch_shapes=[
+            pltpu.VMEM((tokens, features), BF16), pltpu.VMEM((tokens, features), BF16),
+            pltpu.VMEM((tokens, features), BF16), pltpu.VMEM((tokens, features), BF16),
+            pltpu.VMEM((tokens, features), BF16),
+            pltpu.VMEM((blocks // 2, 8, BLOCK), F32), pltpu.VMEM((8, BLOCK), jnp.int32), pltpu.VMEM(slices, BF16),
             pltpu.VMEM(slices, BF16), pltpu.VMEM(eighths, BF16), pltpu.VMEM(eighths, BF16),
             pltpu.VMEM(eighths[1:], BF16), pltpu.VMEM(eighths, BF16), pltpu.VMEM(eighths, BF16),
             pltpu.VMEM(slices, BF16), pltpu.VMEM(slices, F32), pltpu.VMEM(slices, F32),
             pltpu.VMEM(eighths, F32), pltpu.VMEM(eighths, F32), pltpu.VMEM(eighths[1:], F32),
             pltpu.VMEM(eighths, F32),
-            dma((2, 4, 4)), dma((2, 4, 4)), dma((2, 2, 2)), dma((2, 2, 2)),
-            dma((NY, 2)), dma((NY, 2)), dma((7, 8)), dma((7, 8)), dma((6,)),
+            dma((2, 4, 6)), dma((2, 4, 6)), dma((2, 2, 2)), dma((2, 2, 2)),
+            dma((NY, 2)), dma((NY, 2)), dma((7, 8)), dma((7, 8)), dma((11,)),
         ],
         compiler_params=pltpu.CompilerParams(collective_id=0, has_side_effects=True, vmem_limit_bytes=12 * MIB),
         name="gather",
-    )(queries, d_outputs, keys, values, side, refs, cand)
+    )(queries, d_outputs, keys, values, outputs, log_norm, owner, local, glob_blocks)
 
     dq_part, dkv_part = pl.pallas_call(
         functools.partial(pair_kernel, factor=factor),
@@ -645,20 +671,18 @@
             jax.ShapeDtypeStruct((NZ, tokens, features), BF16),
             jax.ShapeDtypeStruct((NY * NC, 2, tokens, features), BF16),
         ),
-        in_specs=[smem, anywhere, anywhere, anywhere, anywhere, vmem],
+        in_specs=[hbm, anywhere, vmem, vmem, vmem, vmem],
         out_specs=(vmem, vmem),
         scratch_shapes=[
             pltpu.VMEM((NZ * blocks + 1, BLOCK, features), F32),
             pltpu.VMEM((NY * NC * blocks + 1, BLOCK, features), F32),
             pltpu.VMEM((NY * NC * blocks + 1, BLOCK, features), F32),
-            pltpu.VMEM((NZ, 2, tokens, features), BF16),
-            pltpu.VMEM((NY * NC, 2, tokens, features), BF16),
-            pltpu.VMEM((NZ, blocks // 2, 8, BLOCK), F32),
+            pltpu.SMEM((2,), jnp.int32),
             pltpu.SMEM((NZ, 8, BLOCK), jnp.int32),
             pltpu.SMEM((256,), jnp.int32),
-            dma((4,)),
+            dma((2,)),
         ],
-        compiler_params=pltpu.CompilerParams(vmem_limit_bytes=32 * MIB),
+        compiler_params=pltpu.CompilerParams(vmem_limit_bytes=16 * MIB),
         name="pairs",
     )(glob_blocks, rf, qd, kv, nd, total)
 

time: 123 us -> 110 us (0.89)
  local copies, waits for them, and re-layouts: 8.86 us -> 2.11 us
  Pallas kernels: 113 us -> 107 us
    pallas_call x1, Pallas kernels: 33.9 us -> 26.6 us  [shards(): pl.pallas_call(functools.partial(reduce_kernel, factor=factor), out_shape...]
    unnamed x19 -> x3, local copies, waits for them, and re-layouts: 8.86 us -> 2.11 us
    pallas_call x1, Pallas kernels: 10.9 us -> 15.7 us  [shards(): pl.pallas_call(functools.partial(pair_kernel, factor=factor), out_shape=(...]
    pallas_call x1 -> x0, Pallas kernels: 2.08 us -> none  [shards(): pl.pallas_call(side_kernel, out_shape=(jax.ShapeDtypeStruct((blocks // 2,...]
    pallas_call x1, Pallas kernels: 66.2 us -> 64.4 us  [shards(): pl.pallas_call(functools.partial(gather_kernel, factor=factor), out_shape...]
where the time goes in v3:
time: 110 us; the launch traced here: 109 us
  Pallas kernels  107 us (97%)
  local copies, waits for them, and re-layouts  2.11 us (2%)
    pallas_call x1, Pallas kernels, shards(): pl.pallas_call(functools.partial(gather_kernel, factor=factor), out_shape...  64.4 us
    pallas_call x1, Pallas kernels, shards(): pl.pallas_call(functools.partial(reduce_kernel, factor=factor), out_shape...  26.6 us
    pallas_call x1, Pallas kernels, shards(): pl.pallas_call(functools.partial(pair_kernel, factor=factor), out_shape=(...  15.7 us

profile of v3, /device:TPU:1, one launch (start us, length us, event | category | flops | bytes accessed | tf_op | source)
XLA Modules:
  0.0 109.5 jit_solution(7214378035983473136)
XLA Ops:
  0.6 64.4 %gather.1 = (bf16[8,2,1024,128]{3,2,1,0:T(8,128)(2,1)S(1)}, bf16[8,2,1024,128]{3,2,1,0:T(8,128)(2,1)S(1)}, f32[8,4,8,128]{3,2,1,0:T(8,128)S(1)}, s32[8,8,128]{2,...) custom-call(bf16[1024,128]{1,0:T(8,128)(2,1)} %q_hbm.1, ...), custom_call_target="tpu_custom_call" | custom-call | tf_op jit(solution)/shard_map/gather/pallas_call | solution.py:637
  65.1 15.7 %pairs.1 = (bf16[8,1024,128]{2,1,0:T(8,128)(2,1)S(1)}, bf16[8,2,1024,128]{3,2,1,0:T(8,128)(2,1)S(1)}) custom-call(s32[2]{0:T(128)} %glob_hbm.1, s32[8,8,128]{2,1,0:T(8,128)S(1)} %get-tuple-element.13.rf_any, bf16[8,2,1024,128]{3,2,1,0:T(8,128)(2,1)S(1)} %get-tuple-element.14.qd_ref, bf16[8,2,1024,128]{3,2,1,0:T(8,128)(2,1)S(1)} %get-tuple-element.15.kv_ref, ...), custom_call_target="tpu_custom_call" | custom-call | tf_op jit(solution)/shard_map/pairs/pallas_call | solution.py:668
  80.8 26.6 %reduce.1 = (bf16[1024,128]{1,0:T(8,128)(2,1)S(1)}, bf16[1024,128]{1,0:T(8,128)(2,1)S(1)}, bf16[1024,128]{1,0:T(8,128)(2,1)S(1)}) custom-call(bf16[8,1024,128]{2,1,0:T(8,128)(2,1)S(1)} %get-tuple-element.18.dq_in, bf16[8,2,1024,128]{3,2,1,0:T(8,128)(2,1)S(1)} %get-tuple-element.19.dkv_in, f32[1024,128]{1,0:T(8,128)S(1)} %get-tuple-element.20.dq_own, ...), custom_call_target="tpu_custom_call" | custom-call | tf_op jit(solution)/shard_map/reduce/pallas_call | solution.py:689
  107.4 0.7 copy.15
  108.1 0.7 copy.16
  108.8 0.7 copy.17

commit v4 on v3

--- a/solution.py
+++ b/solution.py
@@ -60,9 +60,9 @@
 
 def gather_kernel(
     q_hbm, d_hbm, k_hbm, v_hbm, o_hbm, norm_ref, owner_ref, local_ref, glob_ref,
-    qd_out, kv_out, nd_out, rf_out, dq_out, dk_out, dv_out, total_out,
+    qd_out, kv_out, nd_out, rf_out, dq_out, dk_out, dv_out, part_out,
     q_ref, d_ref, k_ref, v_ref, o_ref, nd_ref, rf_ref, cand_ref,
-    g1in, s1, g2in, s2, g3in, s3, gkv, gacc, r1in, t1, r2in, t2, r3in,
+    g1in, s1, g2in, s2, g3in, s3, gkv, gacc, r1in, t1, r2in,
     zsend, zrecv, ysend, yrecv, csend, crecv, gsend, grecv, lsem,
     *, factor,
 ):
@@ -158,7 +158,6 @@
             (gkv.at[me], gkv.at[me]),
             (gacc.at[other], r1in.at[offset]),
             (t1.at[other], r2in.at[offset]),
-            (t2, r3in.at[offset]),
         )[phase]
         return pltpu.make_async_remote_copy(
             src_ref=source,
@@ -271,6 +270,10 @@
     row_values(0)
     small_start(0)
     zstart(1, (1,))
+    for part in (0, 1):
+        for way in (0, 1):
+            ycopy(way, 1, part).start()
+        ccopy(0, part).start()
     for b in range(1, blocks):
         row_values(b)
     loads[4].wait()
@@ -312,61 +315,53 @@
     window(5, 6)
     small_start(2)
     zpass(1, (1, 4, 5))
+    ystep1(0)
     window(6, 9)
     zpass(1, (2,))
+    window(9, 10)
+    zpass(1, (3,))
+    ystep1(1)
+    window(10, 11)
+    zpass(2, (0,))
     small_wait(2)
     s3[z] = s2[...]
     for offset in range(1, 8):
         s3[lax.rem(z + NZ - offset, NZ)] = g3in[offset]
     gkv[me] = s3[...].reshape(gkv.shape[1:])
-    window(9, 11)
+    window(11, 12)
     small_start(3)
-    for part in (0, 1):
-        for way in (0, 1):
-            ycopy(way, 1, part).start()
-        ccopy(0, part).start()
-    zpass(1, (3,))
-    window(11, 14)
-    zpass(2, (0,))
-    small_wait(3)
-    whole(0, 4)
     zpass(2, (1, 4, 5))
-    whole(4, 8)
+    window(12, 16)
     zpass(2, (2,))
-    whole(8, 12)
-    zpass(2, (3,))
-    whole(12, 16)
-    window(14, 15)
-    ystep1(0)
-    small_start(4)
-    zpass(3, (0,))
-    window(15, 17)
-    ystep1(1)
-    small_wait(4)
-    slice_sum = gacc[me]
-    for offset in range(1, 8):
-        slice_sum = slice_sum + r1in[offset]
-    t1[...] = slice_sum.reshape(t1.shape)
-    window(17, 19)
-    small_start(5)
-    zpass(3, (1, 4, 5))
-    window(19, 22)
-    zpass(3, (2,))
-    small_wait(5)
-    part_sum = t1[z]
-    for offset in range(1, 8):
-        part_sum = part_sum + r2in[offset]
-    t2[...] = part_sum
     for way in (0, 1):
         ycopy(way, 2, way).wait_recv()
         ccopy(2, way).start()
-    small_start(6)
+    small_wait(3)
+    whole(0, 4)
+    zpass(2, (3,))
+    whole(4, 10)
+    zpass(3, (0,))
+    whole(10, 16)
+    window(16, 17)
+    small_start(4)
+    zpass(3, (1, 4, 5))
+    window(17, 20)
+    small_wait(4)
+    slice_sum = gacc[me]
+    for offset in range(1, 8):
+        slice_sum = slice_sum + r1in[offset]
+    t1[...] = slice_sum.reshape(t1.shape)
+    window(20, 21)
+    small_start(5)
+    zpass(3, (2,))
+    window(21, 22)
     zpass(3, (3,))
-    small_wait(6)
-    total_out[z] = t2[...]
-    for offset in range(1, 8):
-        total_out[lax.rem(z + NZ - offset, NZ)] = r3in[offset]
-    zpass(4, (0, 1, 4, 5, 2, 3))
+    zpass(4, (0, 2, 1, 4, 5, 3))
+    small_wait(5)
+    part_sum = t1[z]
+    for offset in range(1, 8):
+        part_sum = part_sum + r2in[offset]
+    part_out[...] = part_sum
     for offset in range(NY):
         for part in (0, 1):
             ccopy(offset, part).wait()
@@ -377,7 +372,7 @@
         for part in (0, 1):
             ycopy(way, 1, part).wait_send()
         ycopy(way, 2, way).wait_send()
-    for phase in range(7):
+    for phase in range(6):
         for offset in range(1, 8):
             small(phase, offset).wait_send()
     for copy in local:
@@ -385,19 +380,14 @@
 
 
 def pair_kernel(
-    glob_hbm, rf_any, qd_ref, kv_ref, nd_ref, total_ref, dq_out, dkv_out,
-    dq_acc, dk_acc, dv_acc, glob_ref, rf_ref, list_ref, sem,
+    rf_any, qd_ref, kv_ref, nd_ref, dq_out, dkv_out, dq_acc, dk_acc, dv_acc, rf_ref, list_ref, sem,
     *, factor,
 ):
     y, z, c = place()
     blocks = qd_ref.shape[2] // BLOCK
     grid = NZ * blocks
-    copies = [
-        pltpu.make_async_copy(rf_any, rf_ref, sem.at[0]),
-        pltpu.make_async_copy(glob_hbm, glob_ref, sem.at[1]),
-    ]
-    for copy in copies:
-        copy.start()
+    refs = pltpu.make_async_copy(rf_any, rf_ref, sem)
+    refs.start()
 
     @pl.loop(0, grid)
     def _(i):
@@ -405,25 +395,6 @@
         dq_acc[i] = zero
         dk_acc[i] = zero
         dv_acc[i] = zero
-
-    copies[1].wait()
-    half = BLOCK // 2
-    for g in range(2):
-        owner = glob_ref[g] // blocks
-        column = lax.rem(owner // NC, NZ)
-        member = (owner // (NC * NZ)) * NC + lax.rem(owner, NC)
-        slot = member * blocks + lax.rem(glob_ref[g], blocks)
-        mine = jnp.logical_and(column == z, (y * NC + c) // 4 == g)
-        total = total_ref[...].reshape(half, total_ref.shape[2])
-        rows = pl.ds(pl.multiple_of(c * half, half), half)
-
-        @pl.when(jnp.logical_and(mine, lax.rem(y, 2) == 0))
-        def _():
-            dk_acc[slot, rows, :] += total
-
-        @pl.when(jnp.logical_and(mine, lax.rem(y, 2) == 1))
-        def _():
-            dv_acc[slot, rows, :] += total
 
     def window_item(n, slot, b, seq, key_block, wanted):
         member = (seq // (NC * NZ)) * NC + lax.rem(seq, NC)
@@ -444,7 +415,7 @@
         jnp.clip(far_key, 0, NY * NZ * NC - 1), jnp.where(c == 0, blocks - 1, 0), inside,
     )
 
-    copies[0].wait()
+    refs.wait()
 
     def per_slot(slot, n):
         for b in range(blocks):
@@ -492,24 +463,36 @@
 
 
 def reduce_kernel(
-    dq_in, dkv_in, dq_own, dk_own, dv_own, dq_out, dk_out, dv_out,
-    zbuf, zin, cin, csum, ybuf, yin,
-    zsend, zrecv, ysend, yrecv, csend, crecv,
+    dq_in, dkv_in, dq_own, dk_own, dv_own, part_in, glob_ref, dq_out, dk_out, dv_out,
+    zbuf, zin, cin, ysum, ybuf, yin, rin, totals,
+    zsend, zrecv, ysend, yrecv, csend, crecv, gsend, grecv,
     *, factor,
 ):
     y, z, c = place()
     half = dq_out.shape[0] // 2
+    me = y * NC + c
     zdev = [device(y, lax.rem(z + 1, NZ), c), device(y, lax.rem(z + NZ - 1, NZ), c)]
     ydev = [device(lax.rem(y + 1, NY), z, c), device(lax.rem(y + NY - 1, NY), z, c)]
     cdev = device(y, z, 1 - c)
 
+    def member_device(offset):
+        other = lax.rem(me + offset, NY * NC)
+        return device(other // NC, z, lax.rem(other, NC))
+
+    def row_device(offset):
+        return device(y, lax.rem(z + offset, NZ), c)
+
     barrier = pltpu.get_barrier_semaphore()
-    for target in zdev + ydev + [cdev]:
-        pl.semaphore_signal(barrier, inc=1, device_id=target, device_id_type=MESH)
-    pl.semaphore_wait(barrier, 5)
+    for offset in range(1, 8):
+        for target in (member_device(offset), row_device(offset)):
+            pl.semaphore_signal(barrier, inc=1, device_id=target, device_id_type=MESH)
+    pl.semaphore_wait(barrier, 14)
+
+    def halves(part):
+        return pl.ds(part * half, half)
 
     def zparts(way, step):
-        return (way,) if step == 1 else (0, 1)
+        return (way,) if step == 1 else (1 - way, way)
 
     def zplain(way, step, part):
         return step == 1 or (step == 2 and part != way)
@@ -518,87 +501,136 @@
         return lax.rem(z + (5 - step if way == 0 else NZ - 5 + step), NZ)
 
     def zcopy(way, step, part):
-        rows = pl.ds(part * half, half)
         if zplain(way, step, part):
-            source = dq_in.at[ztarget(way, step), rows]
+            source = dq_in.at[ztarget(way, step), halves(part)]
         else:
-            source = zbuf.at[way, step - 1, rows]
+            source = zbuf.at[way, step - 1, halves(part)]
         return pltpu.make_async_remote_copy(
             src_ref=source,
-            dst_ref=zin.at[way, step - 1, rows],
+            dst_ref=zin.at[way, step - 1, halves(part)],
             send_sem=zsend.at[way, step - 1, part],
             recv_sem=zrecv.at[way, step - 1, part],
             device_id=zdev[way],
             device_id_type=MESH,
         )
 
-    def ccopy(offset, part):
+    def ccopy(offset, part, h):
         row = lax.rem(y + offset, NY)
         return pltpu.make_async_remote_copy(
-            src_ref=dkv_in.at[row * NC + 1 - c, part],
-            dst_ref=cin.at[offset, part],
-            send_sem=csend.at[offset, part],
-            recv_sem=crecv.at[offset, part],
+            src_ref=dkv_in.at[row * NC + 1 - c, part, halves(h)],
+            dst_ref=cin.at[offset, part, halves(h)],
+            send_sem=csend.at[offset, part, h],
+            recv_sem=crecv.at[offset, part, h],
             device_id=cdev,
             device_id_type=MESH,
         )
 
-    def ycopy(way, step, part):
+    def ycopy(way, step, part, h):
         return pltpu.make_async_remote_copy(
-            src_ref=csum.at[2, part] if step == 1 else ybuf.at[way, part],
-            dst_ref=yin.at[way, step - 1, part],
-            send_sem=ysend.at[way, step - 1, part],
-            recv_sem=yrecv.at[way, step - 1, part],
+            src_ref=ysum.at[part, halves(h)] if step == 1 else ybuf.at[way, part, halves(h)],
+            dst_ref=yin.at[way, step - 1, part, halves(h)],
+            send_sem=ysend.at[way, step - 1, part, h],
+            recv_sem=yrecv.at[way, step - 1, part, h],
             device_id=ydev[way],
             device_id_type=MESH,
         )
 
-    for offset in (2, 1, 3, 0):
+    def small(phase, offset):
+        return pltpu.make_async_remote_copy(
+            src_ref=part_in if phase == 0 else totals.at[me],
+            dst_ref=rin.at[offset] if phase == 0 else totals.at[me],
+            send_sem=gsend.at[phase, offset],
+            recv_sem=grecv.at[phase, offset],
+            device_id=row_device(offset) if phase == 0 else member_device(offset),
+            device_id_type=MESH,
+        )
+
+    for h in (0, 1):
         for part in (0, 1):
-            ccopy(offset, part).start()
+            ccopy(2, part, h).start()
+    for offset in range(1, 8):
+        small(0, offset).start()
     for way in (0, 1):
         zcopy(way, 1, way).start()
         zcopy(way, 2, 1 - way).start()
-
-    def zround(step):
+    for h in (0, 1):
+        for way in (0, 1):
+            ccopy(1 if way == 0 else 3, 1 - way, h).start()
+    for h in (0, 1):
+        for way in (0, 1):
+            ccopy(1 if way == 0 else 3, way, h).start()
+    for h in (0, 1):
         for part in (0, 1):
+            ccopy(0, part, h).start()
+
+    def zround(step, late):
+        for way in (0, 1):
+            part = way if late else 1 - way
+            zcopy(way, step, part).wait_recv()
+            rows = halves(part)
+            mine = dq_in[ztarget(way, step + 1), rows, :].astype(F32)
+            zbuf[way, step, rows, :] = (mine + zin[way, step - 1, rows, :].astype(F32)).astype(BF16)
+            zcopy(way, step + 1, part).start()
+
+    def cadd(offset, part, h):
+        ccopy(offset, part, h).wait_recv()
+        row = lax.rem(y + offset, NY)
+        return dkv_in[row * NC + c, part, halves(h), :].astype(F32) + cin[offset, part, halves(h), :].astype(F32)
+
+    def ypass(way, part, h):
+        total = cadd(1 if way == 0 else 3, part, h)
+        if part == way:
+            ycopy(way, 1, part, h).wait_recv()
+            total = total + yin[way, 0, part, halves(h), :].astype(F32)
+        ybuf[way, part, halves(h), :] = total.astype(BF16)
+        ycopy(way, 2, part, h).start()
+
+    for h in (0, 1):
+        for part in (0, 1):
+            ysum[part, halves(h), :] = cadd(2, part, h).astype(BF16)
+            ycopy(part, 1, part, h).start()
+    ypass(0, 1, 0)
+    ypass(1, 0, 0)
+    zround(1, True)
+    ypass(0, 1, 1)
+    ypass(1, 0, 1)
+    for offset in range(1, 8):
+        small(0, offset).wait_recv()
+    totals[me, z] = part_in[...]
+    for offset in range(1, 8):
+        totals[me, lax.rem(z + NZ - offset, NZ)] = rin[offset]
+    ypass(0, 0, 0)
+    ypass(1, 1, 0)
+    zround(2, False)
+    for offset in range(1, 8):
+        small(1, offset).start()
+    zround(2, True)
+    ypass(0, 0, 1)
+    ypass(1, 1, 1)
+    zround(3, False)
+    zround(3, True)
+    for offset in range(1, 8):
+        small(1, offset).wait_recv()
+    seq = lax.axis_index("seq")
+    per_half = half // BLOCK
+    for part, out, own in ((1, dv_out, dv_own), (0, dk_out, dk_own)):
+        for h in (0, 1):
+            total = cadd(0, part, h)
             for way in (0, 1):
-                if part in zparts(way, step):
-                    zcopy(way, step, part).wait_recv()
-                    rows = pl.ds(part * half, half)
-                    mine = dq_in[ztarget(way, step + 1), rows, :].astype(F32)
-                    zbuf[way, step, rows, :] = (mine + zin[way, step - 1, rows, :].astype(F32)).astype(BF16)
-                    zcopy(way, step + 1, part).start()
-
-    def cadd(offset, part):
-        ccopy(offset, part).wait_recv()
-        row = lax.rem(y + offset, NY)
-        mine = dkv_in[row * NC + c, part].astype(F32)
-        return mine + cin[offset, part].astype(F32)
-
+                ycopy(way, 2, part, h).wait_recv()
+                total = total + yin[way, 1, part, halves(h), :].astype(F32)
+            for i in range(per_half):
+                b = h * per_half + i
+                rows = pl.ds(b * BLOCK, BLOCK)
+                more = own[rows, :]
+                for g in range(2):
+                    whole = totals[pl.ds(4 * g + 2 * part, 2)].reshape(more.shape)
+                    more = more + jnp.where(glob_ref[g] == seq * 2 * per_half + b, whole, jnp.zeros_like(whole))
+                if part == 0:
+                    more = more * factor
+                out[rows, :] = (total[i * BLOCK : (i + 1) * BLOCK] + more).astype(BF16)
     for part in (0, 1):
-        csum[2, part] = cadd(2, part).astype(BF16)
-        ycopy(part, 1, part).start()
-    zround(1)
-    for way in (0, 1):
-        offset = 1 if way == 0 else NY - 1
-        for part in (1 - way, way):
-            total = cadd(offset, part)
-            if part == way:
-                ycopy(way, 1, part).wait_recv()
-                total = total + yin[way, 0, part].astype(F32)
-            ybuf[way, part] = total.astype(BF16)
-            ycopy(way, 2, part).start()
-    zround(2)
-    zround(3)
-    for part, out in ((0, dk_out), (1, dv_out)):
-        total = cadd(0, part) + (dk_own[...] * factor if part == 0 else dv_own[...])
-        for way in (0, 1):
-            ycopy(way, 2, part).wait_recv()
-            total = total + yin[way, 1, part].astype(F32)
-        out[...] = total.astype(BF16)
-    for part in (0, 1):
-        rows = pl.ds(part * half, half)
+        rows = halves(part)
         total = dq_in[z, rows, :].astype(F32) + dq_own[rows, :]
         for way in (0, 1):
             zcopy(way, 4, part).wait_recv()
@@ -608,12 +640,17 @@
         for step in range(1, 5):
             for part in zparts(way, step):
                 zcopy(way, step, part).wait_send()
-        ycopy(way, 1, way).wait_send()
-        for part in (0, 1):
-            ycopy(way, 2, part).wait_send()
+        for h in (0, 1):
+            ycopy(way, 1, way, h).wait_send()
+            for part in (0, 1):
+                ycopy(way, 2, part, h).wait_send()
     for offset in range(NY):
         for part in (0, 1):
-            ccopy(offset, part).wait_send()
+            for h in (0, 1):
+                ccopy(offset, part, h).wait_send()
+    for phase in range(2):
+        for offset in range(1, 8):
+            small(phase, offset).wait_send()
 
 
 def shards(queries, keys, values, outputs, d_outputs, log_norm, rand_owner, rand_local, glob_blocks):
@@ -634,7 +671,7 @@
 
     slices = (8, BLOCK // 2, features)
     eighths = (8, BLOCK // 16, features)
-    qd, kv, nd, rf, dq_own, dk_own, dv_own, total = pl.pallas_call(
+    qd, kv, nd, rf, dq_own, dk_own, dv_own, part = pl.pallas_call(
         functools.partial(gather_kernel, factor=factor),
         out_shape=(
             jax.ShapeDtypeStruct((NZ, 2, tokens, features), BF16),
@@ -644,7 +681,7 @@
             jax.ShapeDtypeStruct((tokens, features), F32),
             jax.ShapeDtypeStruct((tokens, features), F32),
             jax.ShapeDtypeStruct((tokens, features), F32),
-            jax.ShapeDtypeStruct(eighths, F32),
+            jax.ShapeDtypeStruct(eighths[1:], F32),
         ),
         in_specs=[hbm] * 5 + [vmem] * 3 + [smem],
         out_specs=(anywhere,) * 4 + (vmem,) * 4,
@@ -656,10 +693,9 @@
             pltpu.VMEM(slices, BF16), pltpu.VMEM(eighths, BF16), pltpu.VMEM(eighths, BF16),
             pltpu.VMEM(eighths[1:], BF16), pltpu.VMEM(eighths, BF16), pltpu.VMEM(eighths, BF16),
             pltpu.VMEM(slices, BF16), pltpu.VMEM(slices, F32), pltpu.VMEM(slices, F32),
-            pltpu.VMEM(eighths, F32), pltpu.VMEM(eighths, F32), pltpu.VMEM(eighths[1:], F32),
-            pltpu.VMEM(eighths, F32),
+            pltpu.VMEM(eighths, F32), pltpu.VMEM(eighths, F32),
             dma((2, 4, 6)), dma((2, 4, 6)), dma((2, 2, 2)), dma((2, 2, 2)),
-            dma((NY, 2)), dma((NY, 2)), dma((7, 8)), dma((7, 8)), dma((11,)),
+            dma((NY, 2)), dma((NY, 2)), dma((6, 8)), dma((6, 8)), dma((11,)),
         ],
         compiler_params=pltpu.CompilerParams(collective_id=0, has_side_effects=True, vmem_limit_bytes=12 * MIB),
         name="gather",
@@ -671,38 +707,40 @@
             jax.ShapeDtypeStruct((NZ, tokens, features), BF16),
             jax.ShapeDtypeStruct((NY * NC, 2, tokens, features), BF16),
         ),
-        in_specs=[hbm, anywhere, vmem, vmem, vmem, vmem],
+        in_specs=[anywhere, vmem, vmem, vmem],
         out_specs=(vmem, vmem),
         scratch_shapes=[
             pltpu.VMEM((NZ * blocks + 1, BLOCK, features), F32),
             pltpu.VMEM((NY * NC * blocks + 1, BLOCK, features), F32),
             pltpu.VMEM((NY * NC * blocks + 1, BLOCK, features), F32),
-            pltpu.SMEM((2,), jnp.int32),
             pltpu.SMEM((NZ, 8, BLOCK), jnp.int32),
             pltpu.SMEM((256,), jnp.int32),
-            dma((2,)),
+            dma,
         ],
         compiler_params=pltpu.CompilerParams(vmem_limit_bytes=16 * MIB),
         name="pairs",
-    )(glob_blocks, rf, qd, kv, nd, total)
+    )(rf, qd, kv, nd)
 
     return tuple(pl.pallas_call(
         functools.partial(reduce_kernel, factor=factor),
         out_shape=(jax.ShapeDtypeStruct((tokens, features), BF16),) * 3,
-        in_specs=[vmem] * 5,
+        in_specs=[vmem] * 6 + [smem],
         out_specs=(vmem,) * 3,
         scratch_shapes=[
             pltpu.VMEM((2, 4, tokens, features), BF16),
             pltpu.VMEM((2, 4, tokens, features), BF16),
             pltpu.VMEM((NY, 2, tokens, features), BF16),
-            pltpu.VMEM((NY, 2, tokens, features), BF16),
+            pltpu.VMEM((2, tokens, features), BF16),
             pltpu.VMEM((2, 2, tokens, features), BF16),
             pltpu.VMEM((2, 2, 2, tokens, features), BF16),
-            dma((2, 4, 2)), dma((2, 4, 2)), dma((2, 2, 2)), dma((2, 2, 2)), dma((NY, 2)), dma((NY, 2)),
+            pltpu.VMEM(eighths, F32),
+            pltpu.VMEM((8,) + eighths, F32),
+            dma((2, 4, 2)), dma((2, 4, 2)), dma((2, 2, 2, 2)), dma((2, 2, 2, 2)),
+            dma((NY, 2, 2)), dma((NY, 2, 2)), dma((2, 8)), dma((2, 8)),
         ],
         compiler_params=pltpu.CompilerParams(collective_id=1, has_side_effects=True, vmem_limit_bytes=24 * MIB),
         name="reduce",
-    )(dq_part, dkv_part, dq_own, dk_own, dv_own))
+    )(dq_part, dkv_part, dq_own, dk_own, dv_own, part, glob_blocks))
 
 
 def solution(mesh):

time: 110 us -> 105 us (0.955)
  Pallas kernels: 107 us -> 102 us
    pallas_call x1, Pallas kernels: 64.4 us -> 58 us  [shards(): pl.pallas_call(functools.partial(gather_kernel, factor=factor), out_shape...]
    pallas_call x1, Pallas kernels: 26.6 us -> 29.2 us  [shards(): pl.pallas_call(functools.partial(reduce_kernel, factor=factor), out_shape...]
where the time goes in v4:
time: 105 us
  Pallas kernels  102 us (97%)
  local copies, waits for them, and re-layouts  2.11 us (2%)
    pallas_call x1, Pallas kernels, shards(): pl.pallas_call(functools.partial(gather_kernel, factor=factor), out_shape...  58 us
    pallas_call x1, Pallas kernels, shards(): pl.pallas_call(functools.partial(reduce_kernel, factor=factor), out_shape...  29.2 us
    pallas_call x1, Pallas kernels, shards(): pl.pallas_call(functools.partial(pair_kernel, factor=factor), out_shape=(...  14.8 us
    unnamed x3, local copies, waits for them, and re-layouts  2.11 us

profile of v4, /device:TPU:1, one launch (start us, length us, event | category | flops | bytes accessed | tf_op | source)
XLA Modules:
  0.0 104.9 jit_solution(2627078782400194501)
XLA Ops:
  0.6 58.0 %gather.1 = (bf16[8,2,1024,128]{3,2,1,0:T(8,128)(2,1)S(1)}, bf16[8,2,1024,128]{3,2,1,0:T(8,128)(2,1)S(1)}, f32[8,4,8,128]{3,2,1,0:T(8,128)S(1)}, s32[8,8,128]{2,...) custom-call(bf16[1024,128]{1,0:T(8,128)(2,1)} %q_hbm.1, ...), custom_call_target="tpu_custom_call" | custom-call | tf_op jit(solution)/shard_map/gather/pallas_call | solution.py:674
  58.7 14.8 %pairs.1 = (bf16[8,1024,128]{2,1,0:T(8,128)(2,1)S(1)}, bf16[8,2,1024,128]{3,2,1,0:T(8,128)(2,1)S(1)}) custom-call(s32[8,8,128]{2,1,0:T(8,128)S(1)} %get-tuple-element.13.rf_any, bf16[8,2,1024,128]{3,2,1,0:T(8,128)(2,1)S(1)} %get-tuple-element.14.qd_ref, bf16[8,2,1024,128]{3,2,1,0:T(8,128)(2,1)S(1)} %get-tuple-element.15.kv_ref, ...), custom_call_target="tpu_custom_call" | custom-call | tf_op jit(solution)/shard_map/pairs/pallas_call | solution.py:704
  73.5 29.2 %reduce.1 = (bf16[1024,128]{1,0:T(8,128)(2,1)S(1)}, bf16[1024,128]{1,0:T(8,128)(2,1)S(1)}, bf16[1024,128]{1,0:T(8,128)(2,1)S(1)}) custom-call(bf16[8,1024,128]{2,1,0:T(8,128)(2,1)S(1)} %get-tuple-element.17.dq_in, bf16[8,2,1024,128]{3,2,1,0:T(8,128)(2,1)S(1)} %get-tuple-element.18.dkv_in, f32[1024,128]{1,0:T(8,128)S(1)} %get-tuple-element.19.dq_own, ...), custom_call_target="tpu_custom_call" | custom-call | tf_op jit(solution)/shard_map/reduce/pallas_call | solution.py:724
  102.8 0.7 copy.15
  103.5 0.7 copy.16
  104.2 0.7 copy.17

commit v5 on v4

--- a/solution.py
+++ b/solution.py
@@ -37,7 +37,6 @@
 
 def pair_terms(q2, d2, nd, k, v, factor):
     k = k * factor
-    rows = k.shape[0]
     across = (((1,), (1,)), ((), ()))
     scores = lax.dot_general(k, q2, across, preferred_element_type=F32)
     grads = lax.dot_general(v, d2, across, preferred_element_type=F32)
@@ -49,8 +48,15 @@
     scores_low = grad_scores.astype(BF16)
     dv = jnp.dot(weights_low, d2, preferred_element_type=F32)
     dk = jnp.dot(scores_low, q2, preferred_element_type=F32)
-    both = jnp.concatenate([scores_low[:, :BLOCK], scores_low[:, BLOCK:]], axis=0)
-    dq = lax.dot_general(both, per_head(k), (((0,), (0,)), ((), ())), preferred_element_type=F32)
+    turned = k.T
+    half = turned.shape[0] // 2
+    dq = jnp.concatenate(
+        [
+            jnp.dot(turned[:half], scores_low[:, :BLOCK], preferred_element_type=F32),
+            jnp.dot(turned[half:], scores_low[:, BLOCK:], preferred_element_type=F32),
+        ],
+        axis=0,
+    )
     return dq, dk, dv
 
 
@@ -61,7 +67,7 @@
 def gather_kernel(
     q_hbm, d_hbm, k_hbm, v_hbm, o_hbm, norm_ref, owner_ref, local_ref, glob_ref,
     qd_out, kv_out, nd_out, rf_out, dq_out, dk_out, dv_out, part_out,
-    q_ref, d_ref, k_ref, v_ref, o_ref, nd_ref, rf_ref, cand_ref,
+    q_ref, d_ref, k_ref, v_ref, o_ref, nd_ref, cand_ref,
     g1in, s1, g2in, s2, g3in, s3, gkv, gacc, r1in, t1, r2in,
     zsend, zrecv, ysend, yrecv, csend, crecv, gsend, grecv, lsem,
     *, factor,
@@ -102,12 +108,12 @@
     def zwhere(part, slot):
         if part < 4:
             return qd_out.at[slot, part // 2, pl.ds((part % 2) * tokens // 2, tokens // 2)]
-        return (nd_out, rf_out)[part - 4].at[slot]
+        return nd_out.at[slot]
 
     def zown(part):
         if part < 4:
             return (q_hbm, d_hbm)[part // 2].at[pl.ds((part % 2) * tokens // 2, tokens // 2)]
-        return (nd_ref, rf_ref)[part - 4]
+        return nd_ref
 
     def zcopy(way, step, part):
         slot = lax.rem(z + (NZ - step + 1 if way == 0 else step - 1), NZ)
@@ -122,8 +128,8 @@
 
     def zparts(way, step):
         if step < 4:
-            return (0, 1, 2, 3, 4, 5)
-        return (0, 1, 4, 5) if way == 0 else (2, 3)
+            return (0, 1, 2, 3, 4)
+        return (0, 1, 4) if way == 0 else (2, 3)
 
     def ycopy(way, step, part):
         row = lax.rem(y + ((NY if step == 1 else NY - 1) if way == 0 else step - 1), NY)
@@ -250,8 +256,8 @@
     owner = owner_ref[...]
     column = jnp.bitwise_and(owner >> 1, NZ - 1)
     other = (owner >> 4) * NC + jnp.bitwise_and(owner, 1)
-    rf_ref[...] = jnp.zeros(rf_ref.shape, jnp.int32)
-    rf_ref[0:3, 0:blocks] = (column * (NY * NC) + other) * blocks + local_ref[...]
+    nd_ref[blocks // 2] = jnp.zeros(nd_ref.shape[1:], F32)
+    nd_ref[blocks // 2, 0:3, 0:blocks] = ((column * (NY * NC) + other) * blocks + local_ref[...]).astype(F32)
     loads[2].wait()
     loads[3].wait()
 
@@ -281,9 +287,8 @@
         pltpu.make_async_copy(q_ref, qd_out.at[z, 0], lsem.at[5]),
         pltpu.make_async_copy(d_ref, qd_out.at[z, 1], lsem.at[6]),
         pltpu.make_async_copy(nd_ref, nd_out.at[z], lsem.at[7]),
-        pltpu.make_async_copy(rf_ref, rf_out.at[z], lsem.at[8]),
-        pltpu.make_async_copy(k_ref, kv_out.at[me, 0], lsem.at[9]),
-        pltpu.make_async_copy(v_ref, kv_out.at[me, 1], lsem.at[10]),
+        pltpu.make_async_copy(k_ref, kv_out.at[me, 0], lsem.at[8]),
+        pltpu.make_async_copy(v_ref, kv_out.at[me, 1], lsem.at[9]),
     ]
     for copy in local:
         copy.start()
@@ -303,7 +308,7 @@
     s1[...] = slice_sum.astype(BF16).reshape(s1.shape)
     window(0, 2)
     small_start(1)
-    zstart(1, (4, 5, 2, 3))
+    zstart(1, (4, 2, 3))
     window(2, 4)
     zpass(1, (0,))
     window(4, 5)
@@ -314,7 +319,7 @@
     s2[...] = part_sum.astype(BF16)
     window(5, 6)
     small_start(2)
-    zpass(1, (1, 4, 5))
+    zpass(1, (1, 4))
     ystep1(0)
     window(6, 9)
     zpass(1, (2,))
@@ -330,7 +335,7 @@
     gkv[me] = s3[...].reshape(gkv.shape[1:])
     window(11, 12)
     small_start(3)
-    zpass(2, (1, 4, 5))
+    zpass(2, (1, 4))
     window(12, 16)
     zpass(2, (2,))
     for way in (0, 1):
@@ -344,7 +349,7 @@
     whole(10, 16)
     window(16, 17)
     small_start(4)
-    zpass(3, (1, 4, 5))
+    zpass(3, (1, 4))
     window(17, 20)
     small_wait(4)
     slice_sum = gacc[me]
@@ -356,7 +361,7 @@
     zpass(3, (2,))
     window(21, 22)
     zpass(3, (3,))
-    zpass(4, (0, 2, 1, 4, 5, 3))
+    zpass(4, (0, 2, 1, 4, 3))
     small_wait(5)
     part_sum = t1[z]
     for offset in range(1, 8):
@@ -377,6 +382,8 @@
             small(phase, offset).wait_send()
     for copy in local:
         copy.wait()
+    for slot in range(NZ):
+        rf_out[slot] = nd_out[slot, blocks // 2].astype(jnp.int32)
 
 
 def pair_kernel(
@@ -388,13 +395,6 @@
     grid = NZ * blocks
     refs = pltpu.make_async_copy(rf_any, rf_ref, sem)
     refs.start()
-
-    @pl.loop(0, grid)
-    def _(i):
-        zero = jnp.zeros((BLOCK, qd_ref.shape[3]), F32)
-        dq_acc[i] = zero
-        dk_acc[i] = zero
-        dv_acc[i] = zero
 
     def window_item(n, slot, b, seq, key_block, wanted):
         member = (seq // (NC * NZ)) * NC + lax.rem(seq, NC)
@@ -418,7 +418,11 @@
     refs.wait()
 
     def per_slot(slot, n):
+        zero = jnp.zeros((BLOCK, qd_ref.shape[3]), F32)
         for b in range(blocks):
+            dq_acc[slot * blocks + b] = zero
+            dk_acc[slot * blocks + b] = zero
+            dv_acc[slot * blocks + b] = zero
             for r in range(3):
                 code = rf_ref[slot, r, b]
                 list_ref[n] = ((slot * blocks + b) << 8) | ((code & (grid - 1)) << 1)
@@ -463,13 +467,13 @@
 
 
 def reduce_kernel(
-    dq_in, dkv_in, dq_own, dk_own, dv_own, part_in, glob_ref, dq_out, dk_out, dv_out,
+    dq_in, dkv_in, dk_own, dv_own, part_in, glob_ref, dq_out, dk_out, dv_out,
     zbuf, zin, cin, ysum, ybuf, yin, rin, totals,
     zsend, zrecv, ysend, yrecv, csend, crecv, gsend, grecv,
     *, factor,
 ):
     y, z, c = place()
-    half = dq_out.shape[0] // 2
+    half = dk_out.shape[0] // 2
     me = y * NC + c
     zdev = [device(y, lax.rem(z + 1, NZ), c), device(y, lax.rem(z + NZ - 1, NZ), c)]
     ydev = [device(lax.rem(y + 1, NY), z, c), device(lax.rem(y + NY - 1, NY), z, c)]
@@ -507,7 +511,7 @@
             source = zbuf.at[way, step - 1, halves(part)]
         return pltpu.make_async_remote_copy(
             src_ref=source,
-            dst_ref=zin.at[way, step - 1, halves(part)],
+            dst_ref=dq_out.at[way, halves(part)] if step == 4 else zin.at[way, step - 1, halves(part)],
             send_sem=zsend.at[way, step - 1, part],
             recv_sem=zrecv.at[way, step - 1, part],
             device_id=zdev[way],
@@ -630,12 +634,8 @@
                     more = more * factor
                 out[rows, :] = (total[i * BLOCK : (i + 1) * BLOCK] + more).astype(BF16)
     for part in (0, 1):
-        rows = halves(part)
-        total = dq_in[z, rows, :].astype(F32) + dq_own[rows, :]
         for way in (0, 1):
             zcopy(way, 4, part).wait_recv()
-            total = total + zin[way, 3, rows, :].astype(F32)
-        dq_out[rows, :] = total.astype(BF16)
     for way in (0, 1):
         for step in range(1, 5):
             for part in zparts(way, step):
@@ -653,6 +653,17 @@
             small(phase, offset).wait_send()
 
 
+def last_kernel(part_ref, own_ref, arrived_ref, dk_in, dv_in, dq_out, dk_out, dv_out):
+    y, z, c = place()
+    for b in range(own_ref.shape[0] // BLOCK):
+        rows = pl.ds(b * BLOCK, BLOCK)
+        total = part_ref[z, rows, :].astype(F32) + own_ref[rows, :]
+        total = total + arrived_ref[0, rows, :].astype(F32) + arrived_ref[1, rows, :].astype(F32)
+        dq_out[rows, :] = total.T.astype(BF16)
+    dk_out[...] = dk_in[...]
+    dv_out[...] = dv_in[...]
+
+
 def shards(queries, keys, values, outputs, d_outputs, log_norm, rand_owner, rand_local, glob_blocks):
     tokens, features = queries.shape
     blocks = tokens // BLOCK
@@ -676,7 +687,7 @@
         out_shape=(
             jax.ShapeDtypeStruct((NZ, 2, tokens, features), BF16),
             jax.ShapeDtypeStruct((NY * NC, 2, tokens, features), BF16),
-            jax.ShapeDtypeStruct((NZ, blocks // 2, 8, BLOCK), F32),
+            jax.ShapeDtypeStruct((NZ, blocks // 2 + 1, 8, BLOCK), F32),
             jax.ShapeDtypeStruct((NZ, 8, BLOCK), jnp.int32),
             jax.ShapeDtypeStruct((tokens, features), F32),
             jax.ShapeDtypeStruct((tokens, features), F32),
@@ -684,18 +695,18 @@
             jax.ShapeDtypeStruct(eighths[1:], F32),
         ),
         in_specs=[hbm] * 5 + [vmem] * 3 + [smem],
-        out_specs=(anywhere,) * 4 + (vmem,) * 4,
+        out_specs=(anywhere,) * 2 + (vmem,) * 6,
         scratch_shapes=[
             pltpu.VMEM((tokens, features), BF16), pltpu.VMEM((tokens, features), BF16),
             pltpu.VMEM((tokens, features), BF16), pltpu.VMEM((tokens, features), BF16),
             pltpu.VMEM((tokens, features), BF16),
-            pltpu.VMEM((blocks // 2, 8, BLOCK), F32), pltpu.VMEM((8, BLOCK), jnp.int32), pltpu.VMEM(slices, BF16),
+            pltpu.VMEM((blocks // 2 + 1, 8, BLOCK), F32), pltpu.VMEM(slices, BF16),
             pltpu.VMEM(slices, BF16), pltpu.VMEM(eighths, BF16), pltpu.VMEM(eighths, BF16),
             pltpu.VMEM(eighths[1:], BF16), pltpu.VMEM(eighths, BF16), pltpu.VMEM(eighths, BF16),
             pltpu.VMEM(slices, BF16), pltpu.VMEM(slices, F32), pltpu.VMEM(slices, F32),
             pltpu.VMEM(eighths, F32), pltpu.VMEM(eighths, F32),
-            dma((2, 4, 6)), dma((2, 4, 6)), dma((2, 2, 2)), dma((2, 2, 2)),
-            dma((NY, 2)), dma((NY, 2)), dma((6, 8)), dma((6, 8)), dma((11,)),
+            dma((2, 4, 5)), dma((2, 4, 5)), dma((2, 2, 2)), dma((2, 2, 2)),
+            dma((NY, 2)), dma((NY, 2)), dma((6, 8)), dma((6, 8)), dma((10,)),
         ],
         compiler_params=pltpu.CompilerParams(collective_id=0, has_side_effects=True, vmem_limit_bytes=12 * MIB),
         name="gather",
@@ -721,14 +732,15 @@
         name="pairs",
     )(rf, qd, kv, nd)
 
-    return tuple(pl.pallas_call(
+    result = jax.ShapeDtypeStruct((tokens, features), BF16)
+    arrived, dk, dv = pl.pallas_call(
         functools.partial(reduce_kernel, factor=factor),
-        out_shape=(jax.ShapeDtypeStruct((tokens, features), BF16),) * 3,
-        in_specs=[vmem] * 6 + [smem],
+        out_shape=(jax.ShapeDtypeStruct((2, tokens, features), BF16), result, result),
+        in_specs=[vmem] * 5 + [smem],
         out_specs=(vmem,) * 3,
         scratch_shapes=[
             pltpu.VMEM((2, 4, tokens, features), BF16),
-            pltpu.VMEM((2, 4, tokens, features), BF16),
+            pltpu.VMEM((2, 3, tokens, features), BF16),
             pltpu.VMEM((NY, 2, tokens, features), BF16),
             pltpu.VMEM((2, tokens, features), BF16),
             pltpu.VMEM((2, 2, tokens, features), BF16),
@@ -740,7 +752,16 @@
         ],
         compiler_params=pltpu.CompilerParams(collective_id=1, has_side_effects=True, vmem_limit_bytes=24 * MIB),
         name="reduce",
-    )(dq_part, dkv_part, dq_own, dk_own, dv_own, part, glob_blocks))
+    )(dq_part, dkv_part, dk_own, dv_own, part, glob_blocks)
+
+    return tuple(pl.pallas_call(
+        last_kernel,
+        out_shape=(result,) * 3,
+        in_specs=[vmem] * 5,
+        out_specs=(vmem,) * 3,
+        compiler_params=pltpu.CompilerParams(vmem_limit_bytes=8 * MIB),
+        name="last",
+    )(dq_part, dq_own, arrived, dk, dv))
 
 
 def solution(mesh):

time: 105 us -> 104 us (level)
  local copies, waits for them, and re-layouts: 2.11 us -> 0 us
    pallas_call x1, Pallas kernels: 29.2 us -> 34.1 us  [shards(): pl.pallas_call(functools.partial(reduce_kernel, factor=factor), out_shape...]
    pallas_call x1, Pallas kernels: 14.8 us -> 10.5 us  [shards(): pl.pallas_call(functools.partial(pair_kernel, factor=factor), out_shape=(...]
    unnamed x3 -> x0, local copies, waits for them, and re-layouts: 2.11 us -> none
where the time goes in v5:
time: 104 us
  Pallas kernels  103 us (99%)
    pallas_call x1, Pallas kernels, shards(): pl.pallas_call(functools.partial(gather_kernel, factor=factor), out_shape...  57.8 us
    pallas_call x1, Pallas kernels, shards(): pl.pallas_call(functools.partial(reduce_kernel, factor=factor), out_shape...  34.1 us
    pallas_call x1, Pallas kernels, shards(): pl.pallas_call(functools.partial(pair_kernel, factor=factor), out_shape=(...  10.5 us

profile of v5, /device:TPU:1, one launch (start us, length us, event | category | flops | bytes accessed | tf_op | source)
XLA Modules:
  0.0 104.1 jit_solution(3101399353570918710)
XLA Ops:
  0.6 57.8 %gather.1 = (bf16[8,2,1024,128]{3,2,1,0:T(8,128)(2,1)S(1)}, bf16[8,2,1024,128]{3,2,1,0:T(8,128)(2,1)S(1)}, f32[8,5,8,128]{3,2,1,0:T(8,128)S(1)}, s32[8,8,128]{2,...) custom-call(bf16[1024,128]{1,0:T(8,128)(2,1)} %q_hbm.1, ...), custom_call_target="tpu_custom_call" | custom-call | tf_op jit(solution)/shard_map/gather/pallas_call | solution.py:685
  58.4 10.5 %pairs.1 = (bf16[8,1024,128]{2,1,0:T(8,128)(2,1)S(1)}, bf16[8,2,1024,128]{3,2,1,0:T(8,128)(2,1)S(1)}) custom-call(s32[8,8,128]{2,1,0:T(8,128)S(1)} %get-tuple-element.16.rf_any, bf16[8,2,1024,128]{3,2,1,0:T(8,128)(2,1)S(1)} %get-tuple-element.17.qd_ref, bf16[8,2,1024,128]{3,2,1,0:T(8,128)(2,1)S(1)} %get-tuple-element.18.kv_ref, ...), custom_call_target="tpu_custom_call" | custom-call | tf_op jit(solution)/shard_map/pairs/pallas_call | solution.py:715
  68.9 34.1 %reduce.1 = (bf16[2,1024,128]{2,1,0:T(8,128)(2,1)S(1)}, bf16[1024,128]{1,0:T(8,128)(2,1)S(1)}, bf16[1024,128]{1,0:T(8,128)(2,1)S(1)}) custom-call(bf16[8,1024,128]{2,1,0:T(8,128)(2,1)S(1)} %get-tuple-element.20.dq_in.part_ref, bf16[8,2,1024,128]{3,2,1,0:T(8,128)(2,1)S(1)} %get-tuple-element.22.dkv_in, f32[1024,128]{1,0:T(8,128)S(1)} %get-tuple-element.23.dk_own, ...), custom_call_target="tpu_custom_call" | custom-call | tf_op jit(solution)/shard_map/reduce/pallas_call | solution.py:736
  103.1 1.0 last.1

commit v6 on v5

--- a/solution.py
+++ b/solution.py
@@ -14,6 +14,7 @@
 F32 = jnp.float32
 BF16 = jnp.bfloat16
 MIB = 1024 * 1024
+STEP = 4
 
 
 def place():
@@ -66,9 +67,9 @@
 
 def gather_kernel(
     q_hbm, d_hbm, k_hbm, v_hbm, o_hbm, norm_ref, owner_ref, local_ref, glob_ref,
-    qd_out, kv_out, nd_out, rf_out, dq_out, dk_out, dv_out, part_out,
+    qd_out, kv_out, nd_out, rf_out, dq_out, dk_out, dv_out, t1,
     q_ref, d_ref, k_ref, v_ref, o_ref, nd_ref, cand_ref,
-    g1in, s1, g2in, s2, g3in, s3, gkv, gacc, r1in, t1, r2in,
+    g1in, s1, g2in, s2, g3in, s3, gkv, gacc, r1in,
     zsend, zrecv, ysend, yrecv, csend, crecv, gsend, grecv, lsem,
     *, factor,
 ):
@@ -163,7 +164,6 @@
             (s2, g3in.at[offset]),
             (gkv.at[me], gkv.at[me]),
             (gacc.at[other], r1in.at[offset]),
-            (t1.at[other], r2in.at[offset]),
         )[phase]
         return pltpu.make_async_remote_copy(
             src_ref=source,
@@ -356,17 +356,10 @@
     for offset in range(1, 8):
         slice_sum = slice_sum + r1in[offset]
     t1[...] = slice_sum.reshape(t1.shape)
-    window(20, 21)
-    small_start(5)
     zpass(3, (2,))
-    window(21, 22)
+    window(20, 22)
     zpass(3, (3,))
     zpass(4, (0, 2, 1, 4, 3))
-    small_wait(5)
-    part_sum = t1[z]
-    for offset in range(1, 8):
-        part_sum = part_sum + r2in[offset]
-    part_out[...] = part_sum
     for offset in range(NY):
         for part in (0, 1):
             ccopy(offset, part).wait()
@@ -377,7 +370,7 @@
         for part in (0, 1):
             ycopy(way, 1, part).wait_send()
         ycopy(way, 2, way).wait_send()
-    for phase in range(6):
+    for phase in range(5):
         for offset in range(1, 8):
             small(phase, offset).wait_send()
     for copy in local:
@@ -430,7 +423,8 @@
         return n
 
     count = lax.fori_loop(0, NZ, per_slot, count)
-    list_ref[count] = jnp.int32(1)
+    for i in range(STEP - 1):
+        list_ref[count + i] = jnp.int32(1)
 
     def terms(item):
         query, key = item >> 8, (item >> 1) & (grid - 1)
@@ -447,9 +441,9 @@
             factor,
         )
 
-    @pl.loop(0, (count + 1) // 2)
+    @pl.loop(0, (count + STEP - 1) // STEP)
     def _(i):
-        items = [list_ref[2 * i], list_ref[2 * i + 1]]
+        items = [list_ref[STEP * i + j] for j in range(STEP)]
         sums = [terms(item) for item in items]
         for item, (dq, dk, dv) in zip(items, sums):
             spare = (item & 1) * grid
@@ -468,7 +462,7 @@
 
 def reduce_kernel(
     dq_in, dkv_in, dk_own, dv_own, part_in, glob_ref, dq_out, dk_out, dv_out,
-    zbuf, zin, cin, ysum, ybuf, yin, rin, totals,
+    zbuf, zin, cin, ysum, ybuf, yin, r2in, t2, rin, totals,
     zsend, zrecv, ysend, yrecv, csend, crecv, gsend, grecv,
     *, factor,
 ):
@@ -540,22 +534,28 @@
         )
 
     def small(phase, offset):
+        source, target = (
+            (part_in.at[lax.rem(z + offset, NZ)], r2in.at[offset]),
+            (t2, rin.at[offset]),
+            (totals.at[me], totals.at[me]),
+        )[phase]
         return pltpu.make_async_remote_copy(
-            src_ref=part_in if phase == 0 else totals.at[me],
-            dst_ref=rin.at[offset] if phase == 0 else totals.at[me],
+            src_ref=source,
+            dst_ref=target,
             send_sem=gsend.at[phase, offset],
             recv_sem=grecv.at[phase, offset],
-            device_id=row_device(offset) if phase == 0 else member_device(offset),
+            device_id=row_device(offset) if phase < 2 else member_device(offset),
             device_id_type=MESH,
         )
 
     for h in (0, 1):
         for part in (0, 1):
             ccopy(2, part, h).start()
+    for way in (0, 1):
+        zcopy(way, 1, way).start()
     for offset in range(1, 8):
         small(0, offset).start()
     for way in (0, 1):
-        zcopy(way, 1, way).start()
         zcopy(way, 2, 1 - way).start()
     for h in (0, 1):
         for way in (0, 1):
@@ -596,25 +596,33 @@
     ypass(0, 1, 0)
     ypass(1, 0, 0)
     zround(1, True)
+    for offset in range(1, 8):
+        small(0, offset).wait_recv()
+    total = part_in[z]
+    for offset in range(1, 8):
+        total = total + r2in[offset]
+    t2[...] = total
     ypass(0, 1, 1)
     ypass(1, 0, 1)
     for offset in range(1, 8):
-        small(0, offset).wait_recv()
-    totals[me, z] = part_in[...]
-    for offset in range(1, 8):
-        totals[me, lax.rem(z + NZ - offset, NZ)] = rin[offset]
+        small(1, offset).start()
     ypass(0, 0, 0)
     ypass(1, 1, 0)
     zround(2, False)
-    for offset in range(1, 8):
-        small(1, offset).start()
     zround(2, True)
     ypass(0, 0, 1)
     ypass(1, 1, 1)
+    for offset in range(1, 8):
+        small(1, offset).wait_recv()
+    totals[me, z] = t2[...]
+    for offset in range(1, 8):
+        totals[me, lax.rem(z + NZ - offset, NZ)] = rin[offset]
     zround(3, False)
+    for offset in range(1, 8):
+        small(2, offset).start()
     zround(3, True)
     for offset in range(1, 8):
-        small(1, offset).wait_recv()
+        small(2, offset).wait_recv()
     seq = lax.axis_index("seq")
     per_half = half // BLOCK
     for part, out, own in ((1, dv_out, dv_own), (0, dk_out, dk_own)):
@@ -648,7 +656,7 @@
         for part in (0, 1):
             for h in (0, 1):
                 ccopy(offset, part, h).wait_send()
-    for phase in range(2):
+    for phase in range(3):
         for offset in range(1, 8):
             small(phase, offset).wait_send()
 
@@ -692,7 +700,7 @@
             jax.ShapeDtypeStruct((tokens, features), F32),
             jax.ShapeDtypeStruct((tokens, features), F32),
             jax.ShapeDtypeStruct((tokens, features), F32),
-            jax.ShapeDtypeStruct(eighths[1:], F32),
+            jax.ShapeDtypeStruct(eighths, F32),
         ),
         in_specs=[hbm] * 5 + [vmem] * 3 + [smem],
         out_specs=(anywhere,) * 2 + (vmem,) * 6,
@@ -704,9 +712,8 @@
             pltpu.VMEM(slices, BF16), pltpu.VMEM(eighths, BF16), pltpu.VMEM(eighths, BF16),
             pltpu.VMEM(eighths[1:], BF16), pltpu.VMEM(eighths, BF16), pltpu.VMEM(eighths, BF16),
             pltpu.VMEM(slices, BF16), pltpu.VMEM(slices, F32), pltpu.VMEM(slices, F32),
-            pltpu.VMEM(eighths, F32), pltpu.VMEM(eighths, F32),
             dma((2, 4, 5)), dma((2, 4, 5)), dma((2, 2, 2)), dma((2, 2, 2)),
-            dma((NY, 2)), dma((NY, 2)), dma((6, 8)), dma((6, 8)), dma((10,)),
+            dma((NY, 2)), dma((NY, 2)), dma((5, 8)), dma((5, 8)), dma((10,)),
         ],
         compiler_params=pltpu.CompilerParams(collective_id=0, has_side_effects=True, vmem_limit_bytes=12 * MIB),
         name="gather",
@@ -746,9 +753,11 @@
             pltpu.VMEM((2, 2, tokens, features), BF16),
             pltpu.VMEM((2, 2, 2, tokens, features), BF16),
             pltpu.VMEM(eighths, F32),
+            pltpu.VMEM(eighths[1:], F32),
+            pltpu.VMEM(eighths, F32),
             pltpu.VMEM((8,) + eighths, F32),
             dma((2, 4, 2)), dma((2, 4, 2)), dma((2, 2, 2, 2)), dma((2, 2, 2, 2)),
-            dma((NY, 2, 2)), dma((NY, 2, 2)), dma((2, 8)), dma((2, 8)),
+            dma((NY, 2, 2)), dma((NY, 2, 2)), dma((3, 8)), dma((3, 8)),
         ],
         compiler_params=pltpu.CompilerParams(collective_id=1, has_side_effects=True, vmem_limit_bytes=24 * MIB),
         name="reduce",

time: 104 us -> 100 us (0.962)
  Pallas kernels: 103 us -> 99.2 us
    pallas_call x1, Pallas kernels: 34.1 us -> 32.4 us  [shards(): pl.pallas_call(functools.partial(reduce_kernel, factor=factor), out_shape...]
    pallas_call x1, Pallas kernels: 10.5 us -> 9.2 us  [shards(): pl.pallas_call(functools.partial(pair_kernel, factor=factor), out_shape=(...]
    pallas_call x1, Pallas kernels: 57.8 us -> 56.6 us  [shards(): pl.pallas_call(functools.partial(gather_kernel, factor=factor), out_shape...]
where the time goes in v6:
time: 100 us; the launch traced here: 99.8 us
  Pallas kernels  99.2 us (99%)
    pallas_call x1, Pallas kernels, shards(): pl.pallas_call(functools.partial(gather_kernel, factor=factor), out_shape...  56.6 us
    pallas_call x1, Pallas kernels, shards(): pl.pallas_call(functools.partial(reduce_kernel, factor=factor), out_shape...  32.4 us
    pallas_call x1, Pallas kernels, shards(): pl.pallas_call(functools.partial(pair_kernel, factor=factor), out_shape=(...  9.2 us

profile of v6, /device:TPU:1, one launch (start us, length us, event | category | flops | bytes accessed | tf_op | source)
XLA Modules:
  0.0 99.8 jit_solution(6788209011236528229)
XLA Ops:
  0.6 56.6 %gather.1 = (bf16[8,2,1024,128]{3,2,1,0:T(8,128)(2,1)S(1)}, bf16[8,2,1024,128]{3,2,1,0:T(8,128)(2,1)S(1)}, f32[8,5,8,128]{3,2,1,0:T(8,128)S(1)}, s32[8,8,128]{2,...) custom-call(bf16[1024,128]{1,0:T(8,128)(2,1)} %q_hbm.1, ...), custom_call_target="tpu_custom_call" | custom-call | tf_op jit(solution)/shard_map/gather/pallas_call | solution.py:693
  57.2 9.2 %pairs.1 = (bf16[8,1024,128]{2,1,0:T(8,128)(2,1)S(1)}, bf16[8,2,1024,128]{3,2,1,0:T(8,128)(2,1)S(1)}) custom-call(s32[8,8,128]{2,1,0:T(8,128)S(1)} %get-tuple-element.16.rf_any, bf16[8,2,1024,128]{3,2,1,0:T(8,128)(2,1)S(1)} %get-tuple-element.17.qd_ref, bf16[8,2,1024,128]{3,2,1,0:T(8,128)(2,1)S(1)} %get-tuple-element.18.kv_ref, ...), custom_call_target="tpu_custom_call" | custom-call | tf_op jit(solution)/shard_map/pairs/pallas_call | solution.py:722
  66.4 32.4 %reduce.1 = (bf16[2,1024,128]{2,1,0:T(8,128)(2,1)S(1)}, bf16[1024,128]{1,0:T(8,128)(2,1)S(1)}, bf16[1024,128]{1,0:T(8,128)(2,1)S(1)}) custom-call(bf16[8,1024,128]{2,1,0:T(8,128)(2,1)S(1)} %get-tuple-element.20.dq_in.part_ref, bf16[8,2,1024,128]{3,2,1,0:T(8,128)(2,1)S(1)} %get-tuple-element.22.dkv_in, f32[1024,128]{1,0:T(8,128)S(1)} %get-tuple-element.23.dk_own, ...), custom_call_target="tpu_custom_call" | custom-call | tf_op jit(solution)/shard_map/reduce/pallas_call | solution.py:743
  98.8 1.0 %last.1 = (bf16[1024,128]{1,0:T(8,128)(2,1)}, bf16[1024,128]{1,0:T(8,128)(2,1)}, bf16[1024,128]{1,0:T(8,128)(2,1)}) custom-call(bf16[8,1024,128]{2,1,0:T(8,128)(2,1)S(1)} %get-tuple-element.20.dq_in.part_ref, f32[1024,128]{1,0:T(8,128)S(1)} %get-tuple-element.21.own_ref, bf16[2,1024,128]{2,1,0:T(8,128)(2,1)S(1)} %get-tuple-element.26.arrived_ref, ...), custom_call_target="tpu_custom_call" | custom-call | tf_op jit(solution)/shard_map/last/pallas_call | solution.py:766

commit v7 on v6

--- a/solution.py
+++ b/solution.py
@@ -355,7 +355,7 @@
     slice_sum = gacc[me]
     for offset in range(1, 8):
         slice_sum = slice_sum + r1in[offset]
-    t1[...] = slice_sum.reshape(t1.shape)
+    t1[...] = slice_sum.astype(BF16).reshape(t1.shape)
     zpass(3, (2,))
     window(20, 22)
     zpass(3, (3,))
@@ -598,10 +598,10 @@
     zround(1, True)
     for offset in range(1, 8):
         small(0, offset).wait_recv()
-    total = part_in[z]
-    for offset in range(1, 8):
-        total = total + r2in[offset]
-    t2[...] = total
+    total = part_in[z].astype(F32)
+    for offset in range(1, 8):
+        total = total + r2in[offset].astype(F32)
+    t2[...] = total.astype(BF16)
     ypass(0, 1, 1)
     ypass(1, 0, 1)
     for offset in range(1, 8):
@@ -612,15 +612,15 @@
     zround(2, True)
     ypass(0, 0, 1)
     ypass(1, 1, 1)
+    zround(3, False)
     for offset in range(1, 8):
         small(1, offset).wait_recv()
     totals[me, z] = t2[...]
     for offset in range(1, 8):
         totals[me, lax.rem(z + NZ - offset, NZ)] = rin[offset]
-    zround(3, False)
+    zround(3, True)
     for offset in range(1, 8):
         small(2, offset).start()
-    zround(3, True)
     for offset in range(1, 8):
         small(2, offset).wait_recv()
     seq = lax.axis_index("seq")
@@ -636,7 +636,7 @@
                 rows = pl.ds(b * BLOCK, BLOCK)
                 more = own[rows, :]
                 for g in range(2):
-                    whole = totals[pl.ds(4 * g + 2 * part, 2)].reshape(more.shape)
+                    whole = totals[pl.ds(4 * g + 2 * part, 2)].astype(F32).reshape(more.shape)
                     more = more + jnp.where(glob_ref[g] == seq * 2 * per_half + b, whole, jnp.zeros_like(whole))
                 if part == 0:
                     more = more * factor
@@ -700,7 +700,7 @@
             jax.ShapeDtypeStruct((tokens, features), F32),
             jax.ShapeDtypeStruct((tokens, features), F32),
             jax.ShapeDtypeStruct((tokens, features), F32),
-            jax.ShapeDtypeStruct(eighths, F32),
+            jax.ShapeDtypeStruct(eighths, BF16),
         ),
         in_specs=[hbm] * 5 + [vmem] * 3 + [smem],
         out_specs=(anywhere,) * 2 + (vmem,) * 6,
@@ -752,10 +752,10 @@
             pltpu.VMEM((2, tokens, features), BF16),
             pltpu.VMEM((2, 2, tokens, features), BF16),
             pltpu.VMEM((2, 2, 2, tokens, features), BF16),
-            pltpu.VMEM(eighths, F32),
-            pltpu.VMEM(eighths[1:], F32),
-            pltpu.VMEM(eighths, F32),
-            pltpu.VMEM((8,) + eighths, F32),
+            pltpu.VMEM(eighths, BF16),
+            pltpu.VMEM(eighths[1:], BF16),
+            pltpu.VMEM(eighths, BF16),
+            pltpu.VMEM((8,) + eighths, BF16),
             dma((2, 4, 2)), dma((2, 4, 2)), dma((2, 2, 2, 2)), dma((2, 2, 2, 2)),
             dma((NY, 2, 2)), dma((NY, 2, 2)), dma((3, 8)), dma((3, 8)),
         ],

time: 100 us -> 98.7 us (0.987)
  Pallas kernels: 99.2 us -> 98.2 us
    pallas_call x1, Pallas kernels: 32.4 us -> 30.4 us  [shards(): pl.pallas_call(functools.partial(reduce_kernel, factor=factor), out_shape...]
    pallas_call x1, Pallas kernels: 9.2 us -> 10.2 us  [shards(): pl.pallas_call(functools.partial(pair_kernel, factor=factor), out_shape=(...]
where the time goes in v7:
time: 98.7 us; the launch traced here: 98.8 us
  Pallas kernels  98.2 us (99%)
    pallas_call x1, Pallas kernels, shards(): pl.pallas_call(functools.partial(gather_kernel, factor=factor), out_shape...  56.6 us
    pallas_call x1, Pallas kernels, shards(): pl.pallas_call(functools.partial(reduce_kernel, factor=factor), out_shape...  30.4 us
    pallas_call x1, Pallas kernels, shards(): pl.pallas_call(functools.partial(pair_kernel, factor=factor), out_shape=(...  10.2 us

profile of v7, /device:TPU:1, one launch (start us, length us, event | category | flops | bytes accessed | tf_op | source)
XLA Modules:
  0.0 98.8 jit_solution(1203507793395698649)
XLA Ops:
  0.6 56.6 %gather.1 = (bf16[8,2,1024,128]{3,2,1,0:T(8,128)(2,1)S(1)}, bf16[8,2,1024,128]{3,2,1,0:T(8,128)(2,1)S(1)}, f32[8,5,8,128]{3,2,1,0:T(8,128)S(1)}, s32[8,8,128]{2,...) custom-call(bf16[1024,128]{1,0:T(8,128)(2,1)} %q_hbm.1, ...), custom_call_target="tpu_custom_call" | custom-call | tf_op jit(solution)/shard_map/gather/pallas_call | solution.py:693
  57.2 10.2 %pairs.1 = (bf16[8,1024,128]{2,1,0:T(8,128)(2,1)S(1)}, bf16[8,2,1024,128]{3,2,1,0:T(8,128)(2,1)S(1)}) custom-call(s32[8,8,128]{2,1,0:T(8,128)S(1)} %get-tuple-element.16.rf_any, bf16[8,2,1024,128]{3,2,1,0:T(8,128)(2,1)S(1)} %get-tuple-element.17.qd_ref, bf16[8,2,1024,128]{3,2,1,0:T(8,128)(2,1)S(1)} %get-tuple-element.18.kv_ref, ...), custom_call_target="tpu_custom_call" | custom-call | tf_op jit(solution)/shard_map/pairs/pallas_call | solution.py:722
  67.4 30.4 %reduce.1 = (bf16[2,1024,128]{2,1,0:T(8,128)(2,1)S(1)}, bf16[1024,128]{1,0:T(8,128)(2,1)S(1)}, bf16[1024,128]{1,0:T(8,128)(2,1)S(1)}) custom-call(bf16[8,1024,128]{2,1,0:T(8,128)(2,1)S(1)} %get-tuple-element.20.dq_in.part_ref, bf16[8,2,1024,128]{3,2,1,0:T(8,128)(2,1)S(1)} %get-tuple-element.22.dkv_in, f32[1024,128]{1,0:T(8,128)S(1)} %get-tuple-element.23.dk_own, ...), custom_call_target="tpu_custom_call" | custom-call | tf_op jit(solution)/shard_map/reduce/pallas_call | solution.py:743
  97.8 1.0 %last.1 = (bf16[1024,128]{1,0:T(8,128)(2,1)}, bf16[1024,128]{1,0:T(8,128)(2,1)}, bf16[1024,128]{1,0:T(8,128)(2,1)}) custom-call(bf16[8,1024,128]{2,1,0:T(8,128)(2,1)S(1)} %get-tuple-element.20.dq_in.part_ref, f32[1024,128]{1,0:T(8,128)S(1)} %get-tuple-element.21.own_ref, bf16[2,1024,128]{2,1,0:T(8,128)(2,1)S(1)} %get-tuple-element.26.arrived_ref, ...), custom_call_target="tpu_custom_call" | custom-call | tf_op jit(solution)/shard_map/last/pallas_call | solution.py:766

commit v8 on v7

--- a/solution.py
+++ b/solution.py
@@ -14,7 +14,7 @@
 F32 = jnp.float32
 BF16 = jnp.bfloat16
 MIB = 1024 * 1024
-STEP = 4
+STEP = 6
 
 
 def place():

time: 98.7 us -> 99.5 us (level)
    pallas_call x1, Pallas kernels: 10.2 us -> 13.3 us  [shards(): pl.pallas_call(functools.partial(pair_kernel, factor=factor), out_shape=(...]
    pallas_call x1, Pallas kernels: 30.4 us -> 27.7 us  [shards(): pl.pallas_call(functools.partial(reduce_kernel, factor=factor), out_shape...]
where the time goes in v8:
time: 99.5 us; the launch traced here: 99.3 us
  Pallas kernels  98.6 us (99%)
    pallas_call x1, Pallas kernels, shards(): pl.pallas_call(functools.partial(gather_kernel, factor=factor), out_shape...  56.6 us
    pallas_call x1, Pallas kernels, shards(): pl.pallas_call(functools.partial(reduce_kernel, factor=factor), out_shape...  27.7 us
    pallas_call x1, Pallas kernels, shards(): pl.pallas_call(functools.partial(pair_kernel, factor=factor), out_shape=(...  13.3 us

profile of v8, /device:TPU:1, one launch (start us, length us, event | category | flops | bytes accessed | tf_op | source)
XLA Modules:
  0.0 99.3 jit_solution(12471818840231775257)
XLA Ops:
  0.6 56.6 %gather.1 = (bf16[8,2,1024,128]{3,2,1,0:T(8,128)(2,1)S(1)}, bf16[8,2,1024,128]{3,2,1,0:T(8,128)(2,1)S(1)}, f32[8,5,8,128]{3,2,1,0:T(8,128)S(1)}, s32[8,8,128]{2,...) custom-call(bf16[1024,128]{1,0:T(8,128)(2,1)} %q_hbm.1, ...), custom_call_target="tpu_custom_call" | custom-call | tf_op jit(solution)/shard_map/gather/pallas_call | solution.py:693
  57.2 13.3 %pairs.1 = (bf16[8,1024,128]{2,1,0:T(8,128)(2,1)S(1)}, bf16[8,2,1024,128]{3,2,1,0:T(8,128)(2,1)S(1)}) custom-call(s32[8,8,128]{2,1,0:T(8,128)S(1)} %get-tuple-element.16.rf_any, bf16[8,2,1024,128]{3,2,1,0:T(8,128)(2,1)S(1)} %get-tuple-element.17.qd_ref, bf16[8,2,1024,128]{3,2,1,0:T(8,128)(2,1)S(1)} %get-tuple-element.18.kv_ref, ...), custom_call_target="tpu_custom_call" | custom-call | tf_op jit(solution)/shard_map/pairs/pallas_call | solution.py:722
  70.5 27.7 %reduce.1 = (bf16[2,1024,128]{2,1,0:T(8,128)(2,1)S(1)}, bf16[1024,128]{1,0:T(8,128)(2,1)S(1)}, bf16[1024,128]{1,0:T(8,128)(2,1)S(1)}) custom-call(bf16[8,1024,128]{2,1,0:T(8,128)(2,1)S(1)} %get-tuple-element.20.dq_in.part_ref, bf16[8,2,1024,128]{3,2,1,0:T(8,128)(2,1)S(1)} %get-tuple-element.22.dkv_in, f32[1024,128]{1,0:T(8,128)S(1)} %get-tuple-element.23.dk_own, ...), custom_call_target="tpu_custom_call" | custom-call | tf_op jit(solution)/shard_map/reduce/pallas_call | solution.py:743
  98.2 1.0 %last.1 = (bf16[1024,128]{1,0:T(8,128)(2,1)}, bf16[1024,128]{1,0:T(8,128)(2,1)}, bf16[1024,128]{1,0:T(8,128)(2,1)}) custom-call(bf16[8,1024,128]{2,1,0:T(8,128)(2,1)S(1)} %get-tuple-element.20.dq_in.part_ref, f32[1024,128]{1,0:T(8,128)S(1)} %get-tuple-element.21.own_ref, bf16[2,1024,128]{2,1,0:T(8,128)(2,1)S(1)} %get-tuple-element.26.arrived_ref, ...), custom_call_target="tpu_custom_call" | custom-call | tf_op jit(solution)/shard_map/last/pallas_call | solution.py:766
